TPU v7x, 256 devices: a whole 4x4x8 slice. The times are simulated.
256 devices in a mesh: img: 16 (over z, core), depth: 16 (over y, x).
Axes of the slice: x: 4, y: 4, z: 8, core: 2. Of those that a mesh axis runs over, the one named last changes fastest.
Arguments:
- volume: bfloat16 [64, 1024, 1024], P('depth', 'img'), may hold values from 0 to 1
- entry_depth: int32 [1024, 1024], P('img'), may hold values from 0 to 63
- tf_table: float32 [256, 4], replicated, may hold values from 0.1 to 4
Outputs:
- image: float32 [4, 1024, 1024], P(None, 'depth', 'img')
All inputs are finite; a program needn't handle non-finite values.
Results may differ from a plain program's by a relative error of at most 0.0003.
Values may be sent and summed in bfloat16 or wider, within the bound.
A program may use at most 64 MiB of HBM per device.

v0:
```python
import math

import jax
import jax.numpy as jnp
from jax import lax
from jax.sharding import PartitionSpec as P


def from_behind(array, axis, by):
    peers = lax.axis_size(axis)
    pairs = [(i, i + by) for i in range(peers) if 0 <= i + by < peers]
    return lax.ppermute(array, axis, pairs)


def partner(block, axis, stride):
    count = lax.axis_size(axis)
    route = []
    for low in range(count):
        high = low | 1 << stride
        if high != low and high < count:
            route += [(low, high), (high, low)]
    return lax.ppermute(block, axis, route)


def table_weights(tf_table):
    bins = tf_table.shape[0]
    following = jnp.concatenate([tf_table[1:], tf_table[-1:]], 0)
    paired = jnp.concatenate([tf_table, following], 1)
    grouped = paired.reshape(bins // 16, 16, 8)
    return jnp.transpose(grouped, (0, 2, 1)).reshape(bins // 16 * 8, 16)


def transfer(sample, pair_weights, bins):
    scaled = sample * (bins - 1)
    lower = jnp.clip(jnp.floor(scaled).astype(jnp.int32), 0, bins - 2)
    frac = scaled - lower.astype(scaled.dtype)
    upper_index = lower // 16
    lower_index = lower - upper_index * 16
    sixteen = lax.broadcasted_iota(jnp.int32, (16,) + (1,) * sample.ndim, 0)
    upper_count = bins // 16
    groups = lax.broadcasted_iota(jnp.int32, (upper_count, 1) + (1,) * sample.ndim, 0)
    onehot_low = (lower_index[None] == sixteen).astype(jnp.float32)
    onehot_high = (upper_index[None, None] == groups).astype(jnp.float32)
    partial_rows = jnp.einsum(
        "ak,kzxr->azxr",
        pair_weights,
        onehot_low,
        precision=lax.Precision.HIGHEST,
        preferred_element_type=jnp.float32,
    )
    partial_rows = partial_rows.reshape((upper_count, 8) + sample.shape)
    values = jnp.sum(partial_rows * onehot_high, axis=0)
    return [
        values[channel_id] + frac * (values[channel_id + 4] - values[channel_id])
        for channel_id in range(4)
    ]


def composite(front_part, back_part):
    return jnp.concatenate(
        [front_part[:3] + front_part[3:4] * back_part[:3], front_part[3:4] * back_part[3:4]], 0
    )


def shards(volume, entry_depth, tf_table):
    slab_depth, block_width, image_rows = volume.shape
    bins = tf_table.shape[0]
    depth_count = lax.axis_size("depth")
    depth_rank = lax.axis_index("depth")
    next_plane = from_behind(volume[0:1], "depth", -1)
    extended = jnp.concatenate([volume, next_plane], 0)
    next_column = from_behind(extended[:, 0:1, :], "img", -1)
    extended = jnp.concatenate([extended, next_column], 1).astype(jnp.float32)
    depth_sum = extended[:-1] + extended[1:]
    column_sum = depth_sum[:, :-1] + depth_sum[:, 1:]
    row_after = jnp.concatenate([column_sum[:, :, 1:], jnp.zeros_like(column_sum[:, :, :1])], 2)
    sample_all = (column_sum + row_after) * 0.125
    pair_weights = table_weights(tf_table)
    row_block = math.gcd(image_rows, 256)
    block_count = image_rows // row_block
    depth_pos = depth_rank * slab_depth + lax.broadcasted_iota(jnp.int32, (slab_depth, 1, 1), 0)
    total_depth = slab_depth * depth_count
    lower_ones = (
        lax.broadcasted_iota(jnp.int32, (slab_depth, slab_depth), 0)
        > lax.broadcasted_iota(jnp.int32, (slab_depth, slab_depth), 1)
    ).astype(jnp.float32)

    def march_block(block_start):
        sample = lax.dynamic_slice_in_dim(sample_all, block_start, row_block, 2)
        entry_block = lax.dynamic_slice_in_dim(entry_depth, block_start, row_block, 1)
        colour = transfer(sample, pair_weights, bins)
        optical = jnp.where(depth_pos >= entry_block[None], colour[3] * (2.0 / total_depth), 0.0)
        opacity = 1.0 - jnp.exp(-optical)
        before = jnp.dot(
            lower_ones,
            optical.reshape(slab_depth, -1),
            precision=lax.Precision.HIGHEST,
            preferred_element_type=jnp.float32,
        ).reshape(optical.shape)
        weight = jnp.exp(-before) * opacity
        planes = [jnp.sum(weight * colour[channel_id], axis=0) for channel_id in range(3)]
        planes.append(jnp.exp(-jnp.sum(optical, axis=0)))
        return jnp.transpose(jnp.stack(planes), (0, 2, 1))

    starts = jnp.arange(block_count, dtype=jnp.int32) * row_block
    blocks = lax.map(march_block, starts)
    brick = jnp.transpose(blocks, (1, 0, 2, 3)).reshape(4, depth_count, -1)
    current = brick
    for level in range(depth_count.bit_length() - 1):
        paired = current.reshape(4, current.shape[1] // 2, 2, current.shape[2])
        front_side = depth_rank >> level & 1 == 0
        lower_half = paired[:, :, 0]
        upper_half = paired[:, :, 1]
        kept_half = jnp.where(front_side, lower_half, upper_half)
        sent_half = jnp.where(front_side, upper_half, lower_half)
        received = partner(sent_half, "depth", level)
        current = jnp.where(
            front_side, composite(kept_half, received), composite(received, kept_half)
        )
    result = current[:, 0]
    return result.reshape(4, -1, block_width)


def solution(mesh):
    placed = (P("depth", "img", None), P("img", None), P())
    return jax.shard_map(
        shards, mesh=mesh, in_specs=placed, out_specs=P(None, "depth", "img"), check_vma=False
    )
```

profile of v0, /device:TPU:38, one launch (start us, length us, event | category | flops | bytes accessed | tf_op | source)
XLA Modules:
  0.0 153.5 jit_solution(8354164549378052895)
XLA Ops:
  0.0 0.9 slice.199
  0.9 2.7 %collective-permute-start = (bf16[1,64,1024]{2,1,0:T(8,128)(2,1)S(1)}, bf16[1,64,1024]{2,1,0:T(8,128)(2,1)S(1)}, u32[]{:S(2)}, u32[]{:S(2)}) collective-permute-start(bf16[1,64,1024]{2,1,0:T(8,128)(2,1)S(1)} %slice.199), channel_id=1, source_target_pairs={{1,0},{2,1},{3,2},{4,3},{5,4},{6,5},{7,6},{8,7},{9,8},{10,9},{11,1... | collective-permute-start | bytes 393224 | tf_op jit(solution)/shard_map/ppermute | solution.py:12
  3.7 0.8 slice.206
  4.4 0.8 slice.207
  5.2 0.8 maximum_maximum_fusion
  5.9 1.1 constant_dynamic-update-slice_fusion.1
  7.0 3.1 %collective-permute-done = bf16[1,64,1024]{2,1,0:T(8,128)(2,1)S(1)} collective-permute-done((bf16[1,64,1024]{2,1,0:T(8,128)(2,1)S(1)}, bf16[1,64,1024]{2,1,0:T(8,128)(2,1)S(1)}, u32[]{:S(2)}, u32[]{:S(2)}) %collective-permute-start) | collective-permute-done | bytes 131104 | tf_op jit(solution)/shard_map/ppermute | solution.py:12
  10.2 1.9 %collective-permute-start.1 = (bf16[5,1,1024]{2,1,0:T(2,128)(2,1)S(1)}, bf16[5,1,1024]{2,1,0:T(2,128)(2,1)S(1)}, u32[]{:S(2)}, u32[]{:S(2)}) collective-permute-start(bf16[5,1,1024]{2,1,0:T(2,128)(2,1)S(1)} %slice.256), channel_id=1, source_target_pairs={{16,0},{32,16},{48,32},{64,48},{80,64},{96,80},{112,96},{128,112},... | collective-permute-start | bytes 30728 | tf_op jit(solution)/shard_map/ppermute | solution.py:12
  12.3 1.3 collective-permute-done.1
  14.6 94.9 %while.13 = (s32[]{:T(128)}, f32[4,4,256,64]{2,3,1,0:T(8,128)S(1)}, s32[4]{0:T(128)S(1)}, s32[64,1024]{1,0:T(8,128)}, f32[4,64,1024]{2,1,0:T(8,128)S(1)}, /*inde...) while((s32[]{:T(128)}, f32[4,4,256,64]{2,3,1,0:T(8,128)S(1)}, ...), condition=%wide.region_6.7_spmd.clone, body=%wide.region_0.6_spmd.clone.sunk | while | flops 1637171200 | bytes 21569740 | solution.py:106
  14.6 0.6 dynamic_slice.48
  17.2 0.6 fusion.59
  17.8 16.1 %fusion.60 = f32[8,4,64,256]{3,0,2,1:T(8,128)S(1)} fusion(f32[16,4,64,256]{3,0,2,1:T(8,128)S(1)} %fusion.59, s32[4,64,256]{2,1,0:T(8,128)S(1)} %get-tuple-element.251, f32[128,16]{0,1:T(8,128)S(1)} %get-tuple-element.289), kind=kOutput, calls=%fused_computation.3.clone.1 | convolution fusion | flops 1627914240 | bytes 6561792 | tf_op jit(solution)/shard_map/while/body/eval_jaxpr/ak,kzxr->azxr/dot_general | solution.py:44
  33.9 2.0 %fusion.61 = (f32[1,4,64,256]{3,0,2,1:T(1,128)S(1)}, f32[1,4,64,256]{3,0,2,1:T(1,128)S(1)}, f32[1,4,64,256]{3,0,2,1:T(1,128)S(1)}, f32[1,4,64,256]{3,0,2,1:T(1,1...) fusion(f32[8,4,64,256]{3,0,2,1:T(8,128)S(1)} %fusion.60), kind=kLoop, calls=%fused_computation.115.clone.1 | loop fusion | bytes 4194304 | tf_op jit(solution)/shard_map/while/body/eval_jaxpr/slice | solution.py:54
  35.9 1.0 constant_dynamic-slice_fusion.2
  37.3 0.6 fusion.63
  37.9 0.4 fusion.64
  38.4 0.6 dynamic_slice.48
  40.9 0.6 fusion.59
  41.5 16.1 %fusion.60 = f32[8,4,64,256]{3,0,2,1:T(8,128)S(1)} fusion(f32[16,4,64,256]{3,0,2,1:T(8,128)S(1)} %fusion.59, s32[4,64,256]{2,1,0:T(8,128)S(1)} %get-tuple-element.251, f32[128,16]{0,1:T(8,128)S(1)} %get-tuple-element.289), kind=kOutput, calls=%fused_computation.3.clone.1 | convolution fusion | flops 1627914240 | bytes 6561792 | tf_op jit(solution)/shard_map/while/body/eval_jaxpr/ak,kzxr->azxr/dot_general | solution.py:44
  57.6 2.0 %fusion.61 = (f32[1,4,64,256]{3,0,2,1:T(1,128)S(1)}, f32[1,4,64,256]{3,0,2,1:T(1,128)S(1)}, f32[1,4,64,256]{3,0,2,1:T(1,128)S(1)}, f32[1,4,64,256]{3,0,2,1:T(1,1...) fusion(f32[8,4,64,256]{3,0,2,1:T(8,128)S(1)} %fusion.60), kind=kLoop, calls=%fused_computation.115.clone.1 | loop fusion | bytes 4194304 | tf_op jit(solution)/shard_map/while/body/eval_jaxpr/slice | solution.py:54
  59.6 1.0 constant_dynamic-slice_fusion.2
  61.0 0.6 fusion.63
  62.1 0.6 dynamic_slice.48
  64.7 0.6 fusion.59
  65.3 16.1 %fusion.60 = f32[8,4,64,256]{3,0,2,1:T(8,128)S(1)} fusion(f32[16,4,64,256]{3,0,2,1:T(8,128)S(1)} %fusion.59, s32[4,64,256]{2,1,0:T(8,128)S(1)} %get-tuple-element.251, f32[128,16]{0,1:T(8,128)S(1)} %get-tuple-element.289), kind=kOutput, calls=%fused_computation.3.clone.1 | convolution fusion | flops 1627914240 | bytes 6561792 | tf_op jit(solution)/shard_map/while/body/eval_jaxpr/ak,kzxr->azxr/dot_general | solution.py:44
  81.4 2.0 %fusion.61 = (f32[1,4,64,256]{3,0,2,1:T(1,128)S(1)}, f32[1,4,64,256]{3,0,2,1:T(1,128)S(1)}, f32[1,4,64,256]{3,0,2,1:T(1,128)S(1)}, f32[1,4,64,256]{3,0,2,1:T(1,1...) fusion(f32[8,4,64,256]{3,0,2,1:T(8,128)S(1)} %fusion.60), kind=kLoop, calls=%fused_computation.115.clone.1 | loop fusion | bytes 4194304 | tf_op jit(solution)/shard_map/while/body/eval_jaxpr/slice | solution.py:54
  83.4 1.0 constant_dynamic-slice_fusion.2
  84.8 0.6 fusion.63
  85.8 0.6 dynamic_slice.48
  88.4 0.6 fusion.59
  89.0 16.1 %fusion.60 = f32[8,4,64,256]{3,0,2,1:T(8,128)S(1)} fusion(f32[16,4,64,256]{3,0,2,1:T(8,128)S(1)} %fusion.59, s32[4,64,256]{2,1,0:T(8,128)S(1)} %get-tuple-element.251, f32[128,16]{0,1:T(8,128)S(1)} %get-tuple-element.289), kind=kOutput, calls=%fused_computation.3.clone.1 | convolution fusion | flops 1627914240 | bytes 6561792 | tf_op jit(solution)/shard_map/while/body/eval_jaxpr/ak,kzxr->azxr/dot_general | solution.py:44
  105.1 2.0 %fusion.61 = (f32[1,4,64,256]{3,0,2,1:T(1,128)S(1)}, f32[1,4,64,256]{3,0,2,1:T(1,128)S(1)}, f32[1,4,64,256]{3,0,2,1:T(1,128)S(1)}, f32[1,4,64,256]{3,0,2,1:T(1,1...) fusion(f32[8,4,64,256]{3,0,2,1:T(8,128)S(1)} %fusion.60), kind=kLoop, calls=%fused_computation.115.clone.1 | loop fusion | bytes 4194304 | tf_op jit(solution)/shard_map/while/body/eval_jaxpr/slice | solution.py:54
  107.1 0.9 constant_dynamic-slice_fusion.2
  108.5 0.6 fusion.63
  109.5 0.6 copy.48
  110.1 1.1 reshape_reshape.3
  111.2 1.3 fusion.41
  113.1 0.6 copy_select_fusion
  113.7 13.1 %collective-permute-done.2 = f32[4,8,4096]{2,1,0:T(8,128)S(1)} collective-permute-done((f32[4,8,4096]{2,1,0:T(8,128)S(1)}, f32[4,8,4096]{2,1,0:T(8,128)S(1)}, u32[]{:S(2)}, u32[]{:S(2)}) %collective-permute-start.2) | collective-permute-done | bytes 524320 | tf_op jit(solution)/shard_map/ppermute | solution.py:22
  127.5 0.4 fusion.33
  127.9 0.6 fusion.42
  129.1 10.2 %collective-permute-done.3 = f32[4,4,4096]{2,1,0:T(4,128)S(1)} collective-permute-done((f32[4,4,4096]{2,1,0:T(4,128)S(1)}, f32[4,4,4096]{2,1,0:T(4,128)S(1)}, u32[]{:S(2)}, u32[]{:S(2)}) %collective-permute-start.3) | collective-permute-done | bytes 262176 | tf_op jit(solution)/shard_map/ppermute | solution.py:22
  140.5 1.7 %collective-permute-start.4 = (f32[4,2,4096]{2,1,0:T(2,128)S(1)}, f32[4,2,4096]{2,1,0:T(2,128)S(1)}, u32[]{:S(2)}, u32[]{:S(2)}) collective-permute-start(f32[4,2,4096]{2,1,0:T(2,128)S(1)} %bitcast.236), channel_id=1, source_target_pairs={{0,4},{4,0},{1,5},{5,1},{2,6},{6,2},{3,7},{7,3},{8,12},{12,8},{9,1... | collective-permute-start | bytes 393224 | tf_op jit(solution)/shard_map/ppermute | solution.py:22
  142.3 3.7 %collective-permute-done.4 = f32[4,2,4096]{2,1,0:T(2,128)S(1)} collective-permute-done((f32[4,2,4096]{2,1,0:T(2,128)S(1)}, f32[4,2,4096]{2,1,0:T(2,128)S(1)}, u32[]{:S(2)}, u32[]{:S(2)}) %collective-permute-start.4) | collective-permute-done | bytes 131104 | tf_op jit(solution)/shard_map/ppermute | solution.py:22
  146.3 3.3 %collective-permute-start.5 = (f32[4,1,4096]{2,1,0:T(1,128)S(1)}, f32[4,1,4096]{2,1,0:T(1,128)S(1)}, u32[]{:S(2)}, u32[]{:S(2)}) collective-permute-start(f32[4,1,4096]{2,1,0:T(1,128)S(1)} %fusion.37), channel_id=1, source_target_pairs={{0,8},{8,0},{1,9},{9,1},{2,10},{10,2},{3,11},{11,3},{4,12},{12,4},... | collective-permute-start | bytes 196616 | tf_op jit(solution)/shard_map/ppermute | solution.py:22
  149.6 2.5 %collective-permute-done.5 = f32[4,1,4096]{2,1,0:T(1,128)S(1)} collective-permute-done((f32[4,1,4096]{2,1,0:T(1,128)S(1)}, f32[4,1,4096]{2,1,0:T(1,128)S(1)}, u32[]{:S(2)}, u32[]{:S(2)}) %collective-permute-start.5) | collective-permute-done | bytes 65568 | tf_op jit(solution)/shard_map/ppermute | solution.py:22
  152.8 0.7 fusion.36
  (72 shorter events, 9.4 us)
Async XLA Ops:
  0.9 9.2 %collective-permute-start = (bf16[1,64,1024]{2,1,0:T(8,128)(2,1)S(1)}, bf16[1,64,1024]{2,1,0:T(8,128)(2,1)S(1)}, u32[]{:S(2)}, u32[]{:S(2)}) collective-permute-start(bf16[1,64,1024]{2,1,0:T(8,128)(2,1)S(1)} %slice.199), channel_id=1, source_target_pairs={{1,0},{2,1},{3,2},{4,3},{5,4},{6,5},{7,6},{8,7},{9,8},{10,9},{11,1... | collective-permute-start | bytes 393224 | tf_op jit(solution)/shard_map/ppermute | solution.py:12
  10.2 3.4 %collective-permute-start.1 = (bf16[5,1,1024]{2,1,0:T(2,128)(2,1)S(1)}, bf16[5,1,1024]{2,1,0:T(2,128)(2,1)S(1)}, u32[]{:S(2)}, u32[]{:S(2)}) collective-permute-start(bf16[5,1,1024]{2,1,0:T(2,128)(2,1)S(1)} %slice.256), channel_id=1, source_target_pairs={{16,0},{32,16},{48,32},{64,48},{80,64},{96,80},{112,96},{128,112},... | collective-permute-start | bytes 30728 | tf_op jit(solution)/shard_map/ppermute | solution.py:12
  112.8 14.0 %collective-permute-start.2 = (f32[4,8,4096]{2,1,0:T(8,128)S(1)}, f32[4,8,4096]{2,1,0:T(8,128)S(1)}, u32[]{:S(2)}, u32[]{:S(2)}) collective-permute-start(f32[4,8,4096]{2,1,0:T(8,128)S(1)} %bitcast.233), channel_id=1, source_target_pairs={{0,1},{1,0},{2,3},{3,2},{4,5},{5,4},{6,7},{7,6},{8,9},{9,8},{10,11... | collective-permute-start | bytes 1572872 | tf_op jit(solution)/shard_map/ppermute | solution.py:22
  128.7 10.7 %collective-permute-start.3 = (f32[4,4,4096]{2,1,0:T(4,128)S(1)}, f32[4,4,4096]{2,1,0:T(4,128)S(1)}, u32[]{:S(2)}, u32[]{:S(2)}) collective-permute-start(f32[4,4,4096]{2,1,0:T(4,128)S(1)} %bitcast.234), channel_id=1, source_target_pairs={{0,2},{2,0},{1,3},{3,1},{4,6},{6,4},{5,7},{7,5},{8,10},{10,8},{9,1... | collective-permute-start | bytes 786440 | tf_op jit(solution)/shard_map/ppermute | solution.py:22
  140.5 5.5 %collective-permute-start.4 = (f32[4,2,4096]{2,1,0:T(2,128)S(1)}, f32[4,2,4096]{2,1,0:T(2,128)S(1)}, u32[]{:S(2)}, u32[]{:S(2)}) collective-permute-start(f32[4,2,4096]{2,1,0:T(2,128)S(1)} %bitcast.236), channel_id=1, source_target_pairs={{0,4},{4,0},{1,5},{5,1},{2,6},{6,2},{3,7},{7,3},{8,12},{12,8},{9,1... | collective-permute-start | bytes 393224 | tf_op jit(solution)/shard_map/ppermute | solution.py:22
  146.3 5.9 %collective-permute-start.5 = (f32[4,1,4096]{2,1,0:T(1,128)S(1)}, f32[4,1,4096]{2,1,0:T(1,128)S(1)}, u32[]{:S(2)}, u32[]{:S(2)}) collective-permute-start(f32[4,1,4096]{2,1,0:T(1,128)S(1)} %fusion.37), channel_id=1, source_target_pairs={{0,8},{8,0},{1,9},{9,1},{2,10},{10,2},{3,11},{11,3},{4,12},{12,4},... | collective-permute-start | bytes 196616 | tf_op jit(solution)/shard_map/ppermute | solution.py:22
where the time goes:
time: 154 us; the launch traced here: 153 us
  matrix products  66.6 us (43%)
  waiting for transfers between devices  33.9 us (22%)
  local copies, waits for them, and re-layouts  22.3 us (14%)
  other arithmetic  13.2 us (9%)
  starting transfers between devices  9.94 us (6%)
  loops' own time  7.1 us (5%)
    dot_general x4, matrix products, transfer(): jnp.einsum('ak,kzxr->azxr', pair_weights, onehot_low, precision=lax.Preci...  64.3 us
    ppermute x4, waiting for transfers between devices, partner(): return lax.ppermute(block, axis, route)  29.5 us
    slice x4, local copies, waits for them, and re-layouts, transfer(): values[channel_id] + frac * (values[channel_id + 4] - values[channel_id])  7.94 us
    another operation x1, loops' own time, shards(): blocks = lax.map(march_block, starts)  7.1 us
    ppermute x4, starting transfers between devices, partner(): return lax.ppermute(block, axis, route)  5.28 us
    ppermute x2, starting transfers between devices, from_behind(): return lax.ppermute(array, axis, pairs)  4.66 us
    ppermute x2, waiting for transfers between devices, from_behind(): return lax.ppermute(array, axis, pairs)  4.4 us
    dynamic_slice x4, local copies, waits for them, and re-layouts, march_block(): lax.dynamic_slice_in_dim(entry_depth, block_start, row_block, 1)  3.86 us
  transfers between devices with their start and end apart: 6, of which 6 were waited for; matrix products, arithmetic and copies ran while one was open for 3% of the time, Pallas kernels for 0%

commit v1 on v0

v1 whole, which is shorter than its diff:
```python
import math

import jax
import jax.numpy as jnp
from jax import lax
from jax.experimental import pallas as pl
from jax.experimental.pallas import tpu as pltpu
from jax.sharding import PartitionSpec as P

MESH = pl.DeviceIdType.MESH
F32, BF16, I32 = jnp.float32, jnp.bfloat16, jnp.int32
ND = 16
NI = 16
ZB = 4
XB = 64
XH = 32
YB = 64
LANES = 128
HALO = 8
BODY = ZB * XH
ROWS = HALO + BODY
KROWS = ROWS + HALO + XH
ORDER = sorted(range(1, ND), key=lambda k: -((0, 1, 2, 1)[k & 3] + (0, 1, 2, 1)[k >> 2]))


def iota(shape, axis):
    return lax.broadcasted_iota(I32, shape, axis)


def zero_one(mask):
    return jnp.where(mask, 1.0, 0.0).astype(BF16)


def nt_dot(a, b, precision=None):
    return lax.dot_general(
        a, b, (((1,), (1,)), ((), ())), preferred_element_type=F32, precision=precision
    )


def halves(a, b, low):
    turned = pltpu.roll(jnp.where(low, b, a), YB, 1)
    return jnp.where(low, a, turned), jnp.where(low, turned, b)


def band_matrix():
    row = iota((BODY, KROWS), 0)
    col = iota((BODY, KROWS), 1)
    z, x = row // XH, row % XH
    nxt = col >= ROWS
    local = jnp.where(nxt, col - ROWS, col)
    is_halo = local < HALO
    zz = jnp.where(nxt, ZB, 0) + jnp.where(is_halo, local, (local - HALO) // XH)
    used = jnp.logical_or(jnp.logical_not(is_halo), local < jnp.where(nxt, 1, ZB))
    xx = jnp.where(is_halo, XH, (local - HALO) % XH)
    dz, dx = zz - z, xx - x
    near = (dz >= 0) & (dz <= 1) & (dx >= 0) & (dx <= 1)
    return zero_one(near & used)


def kernel(
    vol, entry, table, out,
    vbuf, ebuf, cbuf, pk, rb, tabs, edge, ent, band,
    vsem, esem, lsem, csend, crecv, msend, mrecv, hsend, hrecv,
):
    me = lax.axis_index("depth")
    im = lax.axis_index("img")
    left = lax.rem(im + NI - 1, NI)
    right = lax.rem(im + 1, NI)

    barrier = pltpu.get_barrier_semaphore()
    for k in ORDER:
        pl.semaphore_signal(barrier, 1, device_id={"img": im, "depth": me ^ k}, device_id_type=MESH)
    for side in (left, right):
        pl.semaphore_signal(barrier, 1, device_id={"img": side, "depth": me}, device_id_type=MESH)

    load_vol = pltpu.make_async_copy(vol, vbuf, vsem)
    load_vol.start()
    group = pl.multiple_of((me // 2) * LANES, LANES)
    load_entry = pltpu.make_async_copy(entry.at[:, pl.ds(group, LANES)], ebuf, esem)
    load_entry.start()

    low = iota((XH, LANES), 1) < YB
    low8 = iota((8, LANES), 1) < YB

    load_vol.wait()
    for g in range(ND // 2):
        lanes = slice(LANES * g, LANES * (g + 1))
        for z in range(ZB):
            a, b = halves(vbuf[z, 0:XH, lanes], vbuf[z, XH:XB, lanes], low)
            pk[2 * g, HALO + XH * z : HALO + XH * (z + 1), :] = a
            pk[2 * g + 1, HALO + XH * z : HALO + XH * (z + 1), :] = b

    pl.semaphore_wait(barrier, ND - 1 + 2)

    send_col = pltpu.make_async_remote_copy(
        vbuf.at[:, pl.ds(0, 8), :], cbuf, csend, crecv,
        device_id={"img": left, "depth": me}, device_id_type=MESH,
    )
    send_col.start()

    def main_copy(k):
        return pltpu.make_async_remote_copy(
            pk.at[me ^ k, pl.ds(HALO, BODY), :],
            rb.at[me, pl.ds(HALO, BODY), :],
            msend.at[k], mrecv.at[k],
            device_id={"img": im, "depth": me ^ k}, device_id_type=MESH,
        )

    def halo_copy(k):
        return pltpu.make_async_remote_copy(
            pk.at[me ^ k, pl.ds(0, HALO), :],
            rb.at[me, pl.ds(0, HALO), :],
            hsend.at[k], hrecv.at[k],
            device_id={"img": im, "depth": me ^ k}, device_id_type=MESH,
        )

    for k in ORDER:
        main_copy(k).start()

    sel_row = iota((LANES, ND * YB), 0)
    sel_col = iota((LANES, ND * YB), 1)
    hit = sel_col == (sel_row // 8) * YB + YB
    kind = sel_row % 8
    columns = vbuf[...].reshape(ZB * XB, ND * YB)
    rows45 = nt_dot(zero_one(hit & (kind == 4)), columns[:LANES])
    rows45 += nt_dot(zero_one(hit & (kind == 5)), columns[LANES:])
    send_col.wait_recv()
    last = im == NI - 1
    col = [jnp.where(last, 0.0, cbuf[z, 0:1, :].astype(F32)) for z in range(ZB)]
    zero_row = jnp.zeros((1, ND * YB), F32)
    xb = jnp.concatenate(col + [zero_row] * 4, 0)
    xa = jnp.concatenate([vbuf[z, XH : XH + 1, :].astype(F32) for z in range(ZB)] + [zero_row] * 4, 0)
    zcol = iota((LANES, ND * YB), 0)

    def corner_rows(first):
        a = jnp.broadcast_to(col[first], (LANES, ND * YB))
        b = jnp.broadcast_to(col[first + 1], (LANES, ND * YB))
        return jnp.where(zcol == 0, a, jnp.where(zcol == YB, b, 0.0)).astype(BF16)

    rows45 += nt_dot(zero_one(hit & (kind == 6)), corner_rows(0))
    rows45 += nt_dot(zero_one(hit & (kind == 7)), corner_rows(2))
    for g in range(ND // 2):
        lanes = slice(LANES * g, LANES * (g + 1))
        a, b = halves(xa[:, lanes], xb[:, lanes], low8)
        pk[2 * g, 0:HALO, :] = (a + rows45[16 * g : 16 * g + 8]).astype(BF16)
        pk[2 * g + 1, 0:HALO, :] = (b + rows45[16 * g + 8 : 16 * g + 16]).astype(BF16)
    for k in ORDER:
        halo_copy(k).start()
    own = pltpu.make_async_copy(pk.at[me], rb.at[me], lsem)
    own.start()

    rb[ND] = jnp.zeros((ROWS, LANES), BF16)

    eye = jnp.where(iota((8, 4), 0) == iota((8, 4), 1), 1.0, 0.0)
    by_channel = nt_dot(eye, table[...], lax.Precision.HIGHEST)
    lo_half, hi_half = by_channel[:, :LANES], by_channel[:, LANES:]
    last_lane = iota((8, LANES), 1) == LANES - 1
    lo_next = jnp.where(last_lane, pltpu.roll(hi_half, LANES - 1, 1), pltpu.roll(lo_half, LANES - 1, 1))
    lo_next = jnp.where(last_lane, jnp.broadcast_to(hi_half[:, 0:1], (8, LANES)), lo_next)
    hi_next = jnp.where(last_lane, hi_half, pltpu.roll(hi_half, LANES - 1, 1))
    scale = -2.0 / (ND * ZB) * math.log2(math.e)
    for c in range(4):
        for part, rows in enumerate((lo_half, hi_half, lo_next - lo_half, hi_next - hi_half)):
            row = jnp.broadcast_to(rows[c : c + 1], (8, LANES))
            tabs[4 * c + part] = row * scale if c == 3 else row

    band[...] = band_matrix()

    load_entry.wait()
    e0, e1 = ebuf[0:XH, :], ebuf[XH:XB, :]
    even, odd = halves(e0, e1, low)
    ent[...] = jnp.where(lax.rem(me, 2) == 0, even, odd)

    own.wait()
    for k in ORDER:
        main_copy(k).wait_recv()
    for k in ORDER:
        halo_copy(k).wait_recv()

    tiles = jnp.concatenate([rb[d, 0:HALO, :] for d in range(ND)], 0)
    r = iota((LANES, LANES), 0)
    lane = iota((LANES, LANES), 1)
    q, hx = r // 64, r % 64
    dx = lane % 64 - hx
    sums = nt_dot(zero_one((lane // 64 == q) & (dx >= 0) & (dx <= 1)), tiles)
    corner = nt_dot(zero_one((lane == q * 64) & (hx == 63)), tiles)
    sums += pltpu.roll(corner, LANES - 2, 1)
    p0, p1 = sums[:64], sums[64:]
    lane64 = iota((64, LANES), 1)
    nxt = jnp.where(
        lane64 % 8 == 4,
        pltpu.roll(p0, LANES - 1, 1),
        jnp.where(lane64 >= LANES - 7, 0.0, pltpu.roll(p0, LANES - 7, 1)),
    )
    for par, e in enumerate((p0 + p1, p1 + nxt)):
        ea, eb = e[:XH], e[XH:]
        first, second = halves(ea, eb, low)
        edge[par, 0] = first
        edge[par, 1] = second

    is_edge = (iota((8, LANES), 1) & (YB - 1)) == YB - 1
    tiles_x = XH // 8
    zero = jnp.zeros((8, LANES), F32)
    one = jnp.ones((8, LANES), F32)

    def lookup(sample, tab):
        scaled = sample * 31.875
        lower = jnp.minimum(jnp.floor(scaled), 254.0)
        frac = scaled - lower
        index = lower.astype(I32)
        high = index >= LANES
        within = index & (LANES - 1)
        values = []
        for c in range(4):
            t = [jnp.take_along_axis(tab[4 * c + p], within, axis=1, mode="promise_in_bounds") for p in range(4)]
            values.append(jnp.where(high, t[1], t[0]) + frac * jnp.where(high, t[3], t[2]))
        return values

    def brick(d, carry):
        cum, bright, acc = carry
        cum, bright = list(cum), list(bright)
        acc = [list(a) for a in acc]
        data = jnp.concatenate([rb[d], rb[d + 1, 0 : HALO + XH, :]], 0)
        s = jnp.dot(band[...], data, preferred_element_type=F32)
        tab = [tabs[i] for i in range(16)]
        side = d // 8
        base = (d - side * 8) * 8
        for z in range(ZB):
            shift = lax.rem(YB - 1 - (base + 4 + z // 2) + LANES, LANES)
            for t in range(tiles_x):
                here = s[XH * z + 8 * t : XH * z + 8 * t + 8]
                beyond = pltpu.roll(edge[z % 2, side, 8 * t : 8 * t + 8, :], shift, 1)
                below = jnp.where(is_edge, beyond, pltpu.roll(here, LANES - 1, 1))
                colour = lookup(here + below, tab)
                inside = ent[8 * t : 8 * t + 8, :] <= ZB * d + z
                cum[t] = cum[t] + jnp.where(inside, colour[3], 0.0)
                bright_next = jnp.exp2(cum[t])
                weight = bright[t] - bright_next
                bright[t] = bright_next
                for c in range(3):
                    acc[c][t] = acc[c][t] + weight * colour[c]
        return tuple(cum), tuple(bright), tuple(tuple(a) for a in acc)

    start = ((zero,) * tiles_x, (one,) * tiles_x, ((zero,) * tiles_x,) * 3)
    _, bright, acc = lax.fori_loop(0, ND, brick, start)
    planes = jnp.concatenate([v for a in acc for v in a] + list(bright), 0)
    turned = planes.T
    for c in range(4):
        for h in range(2):
            out[c, :, XH * h : XH * (h + 1)] = turned[YB * h : YB * (h + 1), XH * c : XH * (c + 1)]

    for k in ORDER:
        main_copy(k).wait_send()
        halo_copy(k).wait_send()
    send_col.wait_send()


def shards(volume, entry_depth, tf_table):
    dma = pltpu.SemaphoreType.DMA
    return pl.pallas_call(
        kernel,
        out_shape=jax.ShapeDtypeStruct((4, YB, XB), F32),
        in_specs=[
            pl.BlockSpec(memory_space=pl.ANY),
            pl.BlockSpec(memory_space=pl.ANY),
            pl.BlockSpec(memory_space=pltpu.VMEM),
        ],
        out_specs=pl.BlockSpec(memory_space=pltpu.VMEM),
        scratch_shapes=[
            pltpu.VMEM((ZB, XB, ND * YB), BF16),
            pltpu.VMEM((XB, LANES), I32),
            pltpu.VMEM((ZB, 8, ND * YB), BF16),
            pltpu.VMEM((ND, ROWS, LANES), BF16),
            pltpu.VMEM((ND + 1, ROWS, LANES), BF16),
            pltpu.VMEM((16, 8, LANES), F32),
            pltpu.VMEM((2, 2, XH, LANES), F32),
            pltpu.VMEM((XH, LANES), I32),
            pltpu.VMEM((BODY, KROWS), BF16),
            dma, dma, dma, dma, dma,
            dma((ND,)), dma((ND,)), dma((ND,)), dma((ND,)),
        ],
        compiler_params=pltpu.CompilerParams(collective_id=0, has_side_effects=True),
        name="render",
    )(volume, entry_depth, tf_table)


def solution(mesh):
    placed = (P("depth", "img", None), P("img", None), P())
    return jax.shard_map(
        shards, mesh=mesh, in_specs=placed, out_specs=P(None, "depth", "img"), check_vma=False
    )
```

time: 154 us -> 34.5 us (0.22)
  the two profiles are of different devices: /device:TPU:38 before, /device:TPU:97 now
where the time goes in v1:
time: 34.5 us; the launch traced here: 34.4 us
  Pallas kernels  31.3 us (91%)
  local copies, waits for them, and re-layouts  3.05 us (9%)
    pallas_call x1, Pallas kernels, shards(): pl.pallas_call(kernel, out_shape=jax.ShapeDtypeStruct((4, YB, XB), F32),...  31.3 us
    unnamed x2, local copies, waits for them, and re-layouts  3.05 us

profile of v1, /device:TPU:97, one launch (start us, length us, event | category | flops | bytes accessed | tf_op | source)
XLA Modules:
  0.0 34.4 jit_solution(8825006740307778582)
XLA Ops:
  0.0 1.5 %copy.4.table = f32[256,4]{1,0:T(8,128)} copy(f32[256,4]{0,1:T(4,128)} %param.5) | data formatting | bytes 8192 | tf_op args[2]
  1.5 31.3 %render.1 = f32[4,64,64]{2,1,0:T(8,128)} custom-call(bf16[4,64,1024]{2,1,0:T(8,128)(2,1)} %vol.1, s32[64,1024]{1,0:T(8,128)} %entry.1, f32[256,4]{1,0:T(8,128)} %copy.4.table), custom_call_target="tpu_custom_call" | custom-call | tf_op jit(solution)/shard_map/render/pallas_call | solution.py:260
  32.8 1.6 %copy.6 = f32[4,64,64]{2,1,0:T(8,128)} copy(f32[4,64,64]{2,1,0:T(8,128)} %render.1) | data formatting | bytes 131072

commit v2 on v1

v2 whole, which is shorter than its diff:
```python
import math

import jax
import jax.numpy as jnp
from jax import lax
from jax.experimental import pallas as pl
from jax.experimental.pallas import tpu as pltpu
from jax.sharding import PartitionSpec as P

MESH = pl.DeviceIdType.MESH
F32, BF16, I32 = jnp.float32, jnp.bfloat16, jnp.int32
ND = 16
NI = 16
ZB = 4
XB = 64
XH = 32
YB = 64
NY = ND * YB
LANES = 128
TILE = 8
BODY = ZB * XH
ROWS = BODY + TILE
KROWS = BODY + XH + 2 * TILE
XT = XH // 8
SCALE = 255.0 / 8.0
UNIT = 2.0 / 65535.0
OPTICAL = -2.0 / (ND * ZB) * math.log2(math.e) * UNIT * UNIT
ORDER = sorted(range(1, ND), key=lambda k: -((0, 1, 2, 1)[k & 3] + (0, 1, 2, 1)[k >> 2]))


def iota(shape, axis):
    return lax.broadcasted_iota(I32, shape, axis)


def choose(mask, value=1.0):
    return jnp.where(mask, value, 0.0).astype(BF16)


def nt_dot(a, b):
    return lax.dot_general(a, b, (((1,), (1,)), ((), ())), preferred_element_type=F32)


def nn_dot(a, b):
    return jnp.dot(a, b, preferred_element_type=F32)


def halves(a, b, low):
    turned = pltpu.roll(jnp.where(low, b, a), YB, 1)
    return jnp.where(low, a, turned), jnp.where(low, turned, b)


def band_matrix():
    row = iota((BODY, KROWS), 0)
    col = iota((BODY, KROWS), 1)
    z, x = row // XH, row % XH
    tile = col - (BODY + XH)
    in_tile = tile >= 0
    part = tile % TILE - ZB
    zz = jnp.where(in_tile, jnp.where(tile >= TILE, ZB + part, part), col // XH)
    used = (tile < 0) | ((tile < TILE) & (part >= 0)) | ((tile >= TILE) & (part == 0))
    xx = jnp.where(in_tile, XH, col % XH)
    dz, dx = zz - z, xx - x
    near = (dz >= 0) & (dz <= 1) & (dx >= 0) & (dx <= 1)
    return choose(near & used, SCALE)


def kernel(
    vol, entry, table, out,
    vbuf, ebuf, pk, ck, rb, cb, words, ent, band, pair,
    vsem, esem, msend, hsend, csend, mrecv, crecv,
):
    me = lax.axis_index("depth")
    im = lax.axis_index("img")
    left = jnp.maximum(im - 1, 0)
    right = jnp.minimum(im + 1, NI - 1)
    has_left, has_right = im > 0, im < NI - 1

    load_vol = pltpu.make_async_copy(vol, vbuf, vsem)
    load_vol.start()
    group = pl.multiple_of((me // 2) * LANES, LANES)
    load_entry = pltpu.make_async_copy(entry.at[:, pl.ds(group, LANES)], ebuf, esem)
    load_entry.start()

    barrier = pltpu.get_barrier_semaphore()
    for k in ORDER:
        pl.semaphore_signal(barrier, 1, device_id={"img": im, "depth": me ^ k}, device_id_type=MESH)

    @pl.when(has_right)
    def _():
        for k in range(ND):
            pl.semaphore_signal(barrier, 1, device_id={"img": right, "depth": me ^ k}, device_id_type=MESH)

    low = iota((XH, LANES), 1) < YB
    low8 = iota((TILE, LANES), 1) < YB

    load_vol.wait()
    for g in range(ND // 2):
        lanes = slice(LANES * g, LANES * (g + 1))
        for z in range(ZB):
            a, b = halves(vbuf[z, 0:XH, lanes], vbuf[z, XH:XB, lanes], low)
            pk[2 * g, XH * z : XH * (z + 1), :] = a
            pk[2 * g + 1, XH * z : XH * (z + 1), :] = b

    pl.semaphore_wait(barrier, jnp.where(has_left, 2 * ND - 1, ND - 1))

    for k in ORDER:
        pltpu.make_async_remote_copy(
            pk.at[me ^ k, pl.ds(0, BODY), :], rb.at[me, pl.ds(0, BODY), :], msend, mrecv.at[me],
            device_id={"img": im, "depth": me ^ k}, device_id_type=MESH,
        ).start()

    sel = choose(iota((ND, NY), 1) == iota((ND, NY), 0) * YB + YB)
    zero_row = jnp.zeros((1, NY), F32)
    first = jnp.concatenate([vbuf[z, 0:1, :].astype(F32) for z in range(ZB)] + [zero_row] * 4, 0)
    middle = jnp.concatenate([zero_row] * 4 + [vbuf[z, XH : XH + 1, :].astype(F32) for z in range(ZB)], 0)
    by_row = nt_dot(sel, vbuf[...].reshape(ZB * XB, NY)).astype(BF16)
    corner = nt_dot(sel, first.astype(BF16))
    spot = iota((LANES, ND), 0)
    block = iota((LANES, ND), 1)
    lane = iota((LANES, LANES), 1)
    mine = jnp.zeros((LANES, LANES), F32)
    corner = corner.astype(BF16)
    spread = nn_dot(choose(spot // TILE == block), corner)
    at_corner = jnp.zeros((LANES, LANES), F32)
    tile_row = iota((LANES, LANES), 0) % TILE
    for z in range(ZB):
        place = choose((spot // TILE == block) & (spot % TILE == z))
        half = by_row[:, LANES * (z // 2) : LANES * (z // 2 + 1)]
        part = nn_dot(place, half)
        if z % 2:
            part = pltpu.roll(part, YB, 1)
        mine += jnp.where(lane < YB, part, 0.0)
        at_corner += jnp.where((lane == YB) & (tile_row == z), jnp.broadcast_to(spread[:, z : z + 1], (LANES, LANES)), 0.0)
    first = pltpu.roll(first, 4, 0)
    for g in range(ND // 2):
        lanes = slice(LANES * g, LANES * (g + 1))
        a = middle[:, lanes]
        b = first[:, lanes]
        even, odd = slice(2 * TILE * g, 2 * TILE * g + TILE), slice(2 * TILE * g + TILE, 2 * TILE * (g + 1))
        turned = pltpu.roll(jnp.where(low8, b, a), YB, 1)
        pk[2 * g, BODY:ROWS, :] = (mine[even] + jnp.where(low8, a, 0.0)).astype(BF16)
        pk[2 * g + 1, BODY:ROWS, :] = (mine[odd] + jnp.where(low8, turned, 0.0)).astype(BF16)
        ck[2 * g] = (at_corner[even] + jnp.where(low8, 0.0, turned)).astype(BF16)
        ck[2 * g + 1] = (at_corner[odd] + jnp.where(low8, 0.0, b)).astype(BF16)

    for k in ORDER:
        pltpu.make_async_remote_copy(
            pk.at[me ^ k, pl.ds(BODY, TILE), :], rb.at[me, pl.ds(BODY, TILE), :], hsend, mrecv.at[me],
            device_id={"img": im, "depth": me ^ k}, device_id_type=MESH,
        ).start()

    @pl.when(has_left)
    def _():
        for k in range(ND):
            pltpu.make_async_remote_copy(
                ck.at[me ^ k], cb.at[me], csend, crecv.at[me],
                device_id={"img": left, "depth": me ^ k}, device_id_type=MESH,
            ).start()

    pltpu.make_async_copy(pk.at[me], rb.at[me], mrecv.at[me]).start()

    rb[ND] = jnp.zeros((ROWS, LANES), BF16)
    cb[ND] = jnp.zeros((TILE, LANES), BF16)

    @pl.when(jnp.logical_not(has_right))
    def _():
        cb[0:ND] = jnp.zeros((ND, TILE, LANES), BF16)

    code = jnp.floor(jnp.sqrt(table[...]) * (1.0 / UNIT) + 0.5)
    code_lo, code_hi = code[:, :LANES], code[:, LANES:]
    last_lane = iota((4, LANES), 1) == LANES - 1
    turn_lo, turn_hi = pltpu.roll(code_lo, LANES - 1, 1), pltpu.roll(code_hi, LANES - 1, 1)
    next_lo = jnp.where(last_lane, turn_hi, turn_lo)
    next_hi = jnp.where(last_lane, code_hi, turn_hi)
    for half, (a, b) in enumerate(((code_lo, next_lo), (code_hi, next_hi))):
        word = a.astype(I32) | (b.astype(I32) << 16)
        for c in range(4):
            words[2 * c + half] = jnp.broadcast_to(word[c : c + 1], (8, LANES))

    band[...] = band_matrix()
    step = iota((XH, 2 * LANES), 1) % LANES - iota((XH, 2 * LANES), 0)
    pair[...] = choose((step >= 0) & (step <= 1), SCALE)

    load_entry.wait()
    even, odd = halves(ebuf[0:XH, :], ebuf[XH:XB, :], low)
    ent[...] = jnp.where(lax.rem(me, 2) == 0, even, odd)

    is_edge = (iota((8, LANES), 1) & (YB - 1)) == YB - 1
    row8 = iota((TILE, LANES), 0)
    zero = jnp.zeros((8, LANES), F32)
    one = jnp.ones((8, LANES), F32)
    gap = jnp.zeros((YB - TILE, 2 * LANES), F32)

    def arrived(d):
        pltpu.make_async_copy(rb.at[d], rb.at[d], mrecv.at[d]).wait()

        @pl.when(has_right)
        def _():
            pltpu.make_async_copy(cb.at[d], cb.at[d], crecv.at[d]).wait()

    def tile(d):
        return rb[d, BODY:ROWS, :].astype(F32) + cb[d].astype(F32)

    def lookup(scaled):
        lower = jnp.minimum(jnp.floor(scaled), 254.0)
        frac = scaled - lower
        index = lower.astype(I32)
        high = index >= LANES
        within = index & (LANES - 1)
        values = []
        for c in range(4):
            got = [jnp.take_along_axis(words[2 * c + p], within, axis=1, mode="promise_in_bounds") for p in range(2)]
            word = jnp.where(high, got[1], got[0])
            a = (word & 65535).astype(F32)
            b = lax.shift_right_logical(word, jnp.full_like(word, 16)).astype(F32)
            a = a * a
            b = b * b
            values.append(a + frac * (b - a))
        return values

    def brick(d, carry):
        cum, bright, acc = carry
        cum, bright = list(cum), list(bright)
        acc = [list(a) for a in acc]

        @pl.when(d < ND - 1)
        def _():
            arrived(d + 1)

        here, after = tile(d), tile(d + 1)
        data = jnp.concatenate(
            [rb[d, 0:BODY, :], rb[d + 1, 0:XH, :], jnp.concatenate([here, after], 0).astype(BF16)], 0
        )
        s = nn_dot(band[...], data)
        below = jnp.where(row8 == ZB - 1, jnp.broadcast_to(after[0:1], (TILE, LANES)), pltpu.roll(here, TILE - 1, 0))
        two = jnp.concatenate([here, below], 1)
        two_right = jnp.concatenate([pltpu.roll(here, LANES - XH, 1), pltpu.roll(below, LANES - XH, 1)], 1)
        edge = nt_dot(pair[...], jnp.concatenate([two, gap, two_right, gap], 0).astype(BF16))
        for z in range(ZB):
            for t in range(XT):
                value = s[XH * z + 8 * t : XH * z + 8 * t + 8]
                beyond = pltpu.roll(edge[8 * t : 8 * t + 8], YB - 1 - z, 1)
                colour = lookup(value + jnp.where(is_edge, beyond, pltpu.roll(value, LANES - 1, 1)))
                inside = ent[8 * t : 8 * t + 8, :] <= ZB * d + z
                cum[t] = cum[t] + jnp.where(inside, colour[3], 0.0)
                bright_next = jnp.exp2(cum[t] * OPTICAL)
                weight = bright[t] - bright_next
                bright[t] = bright_next
                for c in range(3):
                    acc[c][t] = acc[c][t] + weight * colour[c]
        return tuple(cum), tuple(bright), tuple(tuple(a) for a in acc)

    arrived(0)
    start = ((zero,) * XT, (one,) * XT, ((zero,) * XT,) * 3)
    _, bright, acc = lax.fori_loop(0, ND, brick, start)
    planes = jnp.concatenate([v * (UNIT * UNIT) for a in acc for v in a] + list(bright), 0)
    turned = planes.T
    for c in range(4):
        for h in range(2):
            out[c, :, XH * h : XH * (h + 1)] = turned[YB * h : YB * (h + 1), XH * c : XH * (c + 1)]

    sent = pk.at[pl.ds(0, ND - 1), pl.ds(0, BODY), :]
    pltpu.make_async_copy(sent, sent, msend).wait()
    tiles = pk.at[pl.ds(0, ND - 1), pl.ds(BODY, TILE), :]
    pltpu.make_async_copy(tiles, tiles, hsend).wait()

    @pl.when(has_left)
    def _():
        pltpu.make_async_copy(ck, ck, csend).wait()


def shards(volume, entry_depth, tf_table):
    dma = pltpu.SemaphoreType.DMA
    return pl.pallas_call(
        kernel,
        out_shape=jax.ShapeDtypeStruct((4, YB, XB), F32),
        in_specs=[
            pl.BlockSpec(memory_space=pl.ANY),
            pl.BlockSpec(memory_space=pl.ANY),
            pl.BlockSpec(memory_space=pltpu.VMEM),
        ],
        out_specs=pl.BlockSpec(memory_space=pltpu.VMEM),
        scratch_shapes=[
            pltpu.VMEM((ZB, XB, NY), BF16),
            pltpu.VMEM((XB, LANES), I32),
            pltpu.VMEM((ND, ROWS, LANES), BF16),
            pltpu.VMEM((ND, TILE, LANES), BF16),
            pltpu.VMEM((ND + 1, ROWS, LANES), BF16),
            pltpu.VMEM((ND + 1, TILE, LANES), BF16),
            pltpu.VMEM((8, 8, LANES), I32),
            pltpu.VMEM((XH, LANES), I32),
            pltpu.VMEM((BODY, KROWS), BF16),
            pltpu.VMEM((XH, 2 * LANES), BF16),
            dma, dma, dma, dma, dma,
            dma((ND,)), dma((ND,)),
        ],
        compiler_params=pltpu.CompilerParams(collective_id=0, has_side_effects=True),
        name="render",
    )(volume, entry_depth, tf_table.T)


def solution(mesh):
    placed = (P("depth", "img", None), P("img", None), P())
    return jax.shard_map(
        shards, mesh=mesh, in_specs=placed, out_specs=P(None, "depth", "img"), check_vma=False
    )
```

time: 34.5 us -> 26.3 us (0.76)
  the two profiles are of different devices: /device:TPU:97 before, /device:TPU:1 now
where the time goes in v2:
time: 26.3 us; the launch traced here: 26.1 us
  Pallas kernels  24.6 us (94%)
  local copies, waits for them, and re-layouts  1.57 us (6%)
    pallas_call x1, Pallas kernels, shards(): pl.pallas_call(kernel, out_shape=jax.ShapeDtypeStruct((4, YB, XB), F32),...  24.6 us
    unnamed x1, local copies, waits for them, and re-layouts  1.57 us

profile of v2, /device:TPU:1, one launch (start us, length us, event | category | flops | bytes accessed | tf_op | source)
XLA Modules:
  0.0 26.1 jit_solution(5886842572576217170)
XLA Ops:
  0.0 24.6 %render.1 = f32[4,64,64]{2,1,0:T(8,128)} custom-call(bf16[4,64,1024]{2,1,0:T(8,128)(2,1)} %vol.1, s32[64,1024]{1,0:T(8,128)} %entry.1, f32[4,256]{1,0:T(4,128)} %bitcast.1), custom_call_target="tpu_custom_call" | custom-call | tf_op jit(solution)/shard_map/render/pallas_call | solution.py:274
  24.6 1.6 %copy.5 = f32[4,64,64]{2,1,0:T(8,128)} copy(f32[4,64,64]{2,1,0:T(8,128)} %render.1) | data formatting | bytes 131072

commit v3 on v2

v3 whole, which is shorter than its diff:
```python
import math

import jax
import jax.numpy as jnp
from jax import lax
from jax.experimental import pallas as pl
from jax.experimental.pallas import tpu as pltpu
from jax.sharding import PartitionSpec as P

MESH = pl.DeviceIdType.MESH
F32, BF16, I32 = jnp.float32, jnp.bfloat16, jnp.int32
ND = 16
NI = 16
ZB = 4
XB = 64
XH = 32
YB = 64
NY = ND * YB
LANES = 128
TILE = 8
BODY = ZB * XH
ROWS = BODY + TILE
KROWS = BODY + XH + 2 * TILE
XT = XH // 8
SCALE = 255.0 / 8.0
UNIT = 2.0 / 65535.0
OPTICAL = -2.0 / (ND * ZB) * math.log2(math.e) * UNIT * UNIT
EARLY = 2


def iota(shape, axis):
    return lax.broadcasted_iota(I32, shape, axis)


def choose(mask, value=1.0):
    return jnp.where(mask, value, 0.0).astype(BF16)


def nt_dot(a, b):
    return lax.dot_general(a, b, (((1,), (1,)), ((), ())), preferred_element_type=F32)


def nn_dot(a, b):
    return jnp.dot(a, b, preferred_element_type=F32)


def halves(a, b, low):
    turned = pltpu.roll(jnp.where(low, b, a), YB, 1)
    return jnp.where(low, a, turned), jnp.where(low, turned, b)


def band_matrix():
    row = iota((BODY, KROWS), 0)
    col = iota((BODY, KROWS), 1)
    z, x = row // XH, row % XH
    tile = col - (BODY + XH)
    in_tile = tile >= 0
    part = tile % TILE - ZB
    zz = jnp.where(in_tile, jnp.where(tile >= TILE, ZB + part, part), col // XH)
    used = (tile < 0) | ((tile < TILE) & (part >= 0)) | ((tile >= TILE) & (part == 0))
    xx = jnp.where(in_tile, XH, col % XH)
    dz, dx = zz - z, xx - x
    near = (dz >= 0) & (dz <= 1) & (dx >= 0) & (dx <= 1)
    return choose(near & used, SCALE)


def kernel(
    vol, entry, table, out,
    vbuf, ebuf, pk, ck, rb, cb, words, ent, band, pair, state, behind, sbuf,
    vsem, esem, msend, hsend, csend, mrecv, crecv,
):
    me = lax.axis_index("depth")
    im = lax.axis_index("img")
    base = me & (ND - 2)
    left = jnp.maximum(im - 1, 0)
    right = jnp.minimum(im + 1, NI - 1)
    has_left, has_right = im > 0, im < NI - 1

    load_vol = pltpu.make_async_copy(vol, vbuf, vsem)
    load_vol.start()
    group = pl.multiple_of((me // 2) * LANES, LANES)
    load_entry = pltpu.make_async_copy(entry.at[:, pl.ds(group, LANES)], ebuf, esem)
    load_entry.start()

    barrier = pltpu.get_barrier_semaphore()
    for k in range(1, ND):
        pl.semaphore_signal(barrier, 1, device_id={"img": im, "depth": me ^ k}, device_id_type=MESH)

    @pl.when(has_right)
    def _():
        for k in range(ND):
            pl.semaphore_signal(barrier, 1, device_id={"img": right, "depth": me ^ k}, device_id_type=MESH)

    low = iota((XH, LANES), 1) < YB
    low8 = iota((TILE, LANES), 1) < YB

    load_vol.wait()
    for g in range(ND // 2):
        lanes = slice(LANES * g, LANES * (g + 1))
        for z in range(ZB):
            a, b = halves(vbuf[z, 0:XH, lanes], vbuf[z, XH:XB, lanes], low)
            pk[2 * g, XH * z : XH * (z + 1), :] = a
            pk[2 * g + 1, XH * z : XH * (z + 1), :] = b

    pl.semaphore_wait(barrier, jnp.where(has_left, 2 * ND - 1, ND - 1))

    def target_of(step):
        return (me ^ 1) if step == 0 else (base - step // 2 * 2 + step % 2) & (ND - 1)

    def send(step, first, rows, sem):
        target = target_of(step)
        return pltpu.make_async_remote_copy(
            pk.at[target, pl.ds(first, rows), :], rb.at[me, pl.ds(first, rows), :], sem, mrecv.at[me],
            device_id={"img": im, "depth": target}, device_id_type=MESH,
        )

    steps = [0] + list(range(2, ND))
    for step in steps[:EARLY]:
        send(step, 0, BODY, hsend).start()

    sel = choose(iota((ND, NY), 1) == iota((ND, NY), 0) * YB + YB)
    zero_row = jnp.zeros((1, NY), F32)
    pad = jnp.zeros((ND, LANES - XB), F32)
    by_row = [jnp.concatenate([nt_dot(sel, vbuf[z]), pad], 1) for z in range(ZB)]
    spot = iota((LANES, ZB * ND), 0)
    block = iota((LANES, ZB * ND), 1)
    place = choose((spot // TILE == block % ND) & (spot % TILE == block // ND))
    mine = nn_dot(place, jnp.concatenate(by_row, 0).astype(BF16))
    middle = jnp.concatenate([zero_row] * 4 + [vbuf[z, XH : XH + 1, :].astype(F32) for z in range(ZB)], 0)
    for g in range(ND // 2):
        a = middle[:, LANES * g : LANES * (g + 1)]
        turned = pltpu.roll(a, YB, 1)
        at = 2 * TILE * g
        pk[2 * g, BODY:ROWS, :] = (mine[at : at + TILE] + jnp.where(low8, a, 0.0)).astype(BF16)
        pk[2 * g + 1, BODY:ROWS, :] = (mine[at + TILE : at + 2 * TILE] + jnp.where(low8, turned, 0.0)).astype(BF16)

    for step in steps[:EARLY]:
        send(step, BODY, TILE, hsend).start()
    for step in steps[EARLY:]:
        send(step, 0, ROWS, msend).start()
    pltpu.make_async_copy(pk.at[me], rb.at[me], mrecv.at[me]).start()

    first = jnp.concatenate([vbuf[z, 0:1, :].astype(F32) for z in range(ZB)] + [zero_row] * 4, 0)
    corner = nt_dot(sel, first.astype(BF16)).astype(BF16)
    spot16 = iota((LANES, ND), 0)
    spread = nn_dot(choose(spot16 // TILE == iota((LANES, ND), 1)), corner)
    lane8 = iota((LANES, TILE), 1)
    spread = jnp.sum(jnp.where(lane8 == iota((LANES, TILE), 0) % TILE, spread, 0.0), 1, keepdims=True)
    lane = iota((LANES, LANES), 1)
    at_corner = jnp.where((lane == YB) & (iota((LANES, LANES), 0) % TILE < ZB), jnp.broadcast_to(spread, (LANES, LANES)), 0.0)
    first = pltpu.roll(first, 4, 0)
    for g in range(ND // 2):
        a = first[:, LANES * g : LANES * (g + 1)]
        turned = pltpu.roll(a, YB, 1)
        at = 2 * TILE * g
        ck[2 * g] = (at_corner[at : at + TILE] + jnp.where(low8, 0.0, turned)).astype(BF16)
        ck[2 * g + 1] = (at_corner[at + TILE : at + 2 * TILE] + jnp.where(low8, 0.0, a)).astype(BF16)

    @pl.when(has_left)
    def _():
        for step in range(ND):
            target = (base - step // 2 * 2 + step % 2) & (ND - 1)
            pltpu.make_async_remote_copy(
                ck.at[target], cb.at[me], csend, crecv.at[me],
                device_id={"img": left, "depth": target}, device_id_type=MESH,
            ).start()

    rb[ND] = jnp.zeros((ROWS, LANES), BF16)
    cb[ND] = jnp.zeros((TILE, LANES), BF16)

    @pl.when(jnp.logical_not(has_right))
    def _():
        cb[0:ND] = jnp.zeros((ND, TILE, LANES), BF16)

    code = jnp.floor(jnp.sqrt(table[...]) * (1.0 / UNIT) + 0.5)
    code = jnp.concatenate([code, code], 0).astype(I32)
    lane128 = iota((8, LANES), 1)
    even_of = (2 * lane128) & (LANES - 1)

    def every_other(offset):
        lo, hi = (
            jnp.take_along_axis(part, even_of + offset, axis=1, mode="promise_in_bounds")
            for part in (code[:, :LANES], code[:, LANES:])
        )
        return jnp.where(lane128 < LANES // 2, lo, hi)

    even_code, odd_code = every_other(0), every_other(1)
    next_code = pltpu.roll(even_code, LANES - 1, 1)
    for c in range(4):
        words[c] = jnp.broadcast_to((even_code | (odd_code << 16))[c : c + 1], (8, LANES))
    for p in range(2):
        word = next_code[2 * p : 2 * p + 1] | (next_code[2 * p + 1 : 2 * p + 2] << 16)
        words[4 + p] = jnp.broadcast_to(word, (8, LANES))

    band[...] = band_matrix()
    step = iota((XH, 2 * LANES), 1) % LANES - iota((XH, 2 * LANES), 0)
    pair[...] = choose((step >= 0) & (step <= 1), SCALE)

    load_entry.wait()
    even, odd = halves(ebuf[0:XH, :], ebuf[XH:XB, :], low)
    ent[...] = jnp.where(lax.rem(me, 2) == 0, even, odd)

    is_edge = (iota((8, LANES), 1) & (YB - 1)) == YB - 1
    row8 = iota((TILE, LANES), 0)
    zero = jnp.zeros((8, LANES), F32)
    one = jnp.ones((8, LANES), F32)
    gap = jnp.zeros((YB - TILE, 2 * LANES), F32)

    def arrived(d):
        pltpu.make_async_copy(rb.at[d], rb.at[d], mrecv.at[d]).wait()

        @pl.when(has_right)
        def _():
            pltpu.make_async_copy(cb.at[d], cb.at[d], crecv.at[d]).wait()

    def tile(d):
        return rb[d, BODY:ROWS, :].astype(F32) + cb[d].astype(F32)

    def lookup(scaled):
        lower = jnp.minimum(jnp.floor(scaled), 254.0)
        frac = scaled - lower
        index = lower.astype(I32)
        odd = (index & 1) == 1
        within = lax.shift_right_logical(index, jnp.full_like(index, 1))

        def get(i):
            return jnp.take_along_axis(words[i], within, axis=1, mode="promise_in_bounds")

        values = []
        beyond = (get(4), get(5))
        for c in range(4):
            word = get(c)
            a = word & 65535
            b = lax.shift_right_logical(word, jnp.full_like(word, 16))
            e = beyond[c // 2]
            e = lax.shift_right_logical(e, jnp.full_like(e, 16)) if c % 2 else e & 65535
            lo = jnp.where(odd, b, a).astype(F32)
            hi = jnp.where(odd, e, b).astype(F32)
            lo = lo * lo
            hi = hi * hi
            values.append(lo + frac * (hi - lo))
        return values

    def sums(d):
        here, after = tile(d), tile(d + 1)
        data = jnp.concatenate(
            [rb[d, 0:BODY, :], rb[d + 1, 0:XH, :], jnp.concatenate([here, after], 0).astype(BF16)], 0
        )
        below = jnp.where(row8 == ZB - 1, jnp.broadcast_to(after[0:1], (TILE, LANES)), pltpu.roll(here, TILE - 1, 0))
        two = jnp.concatenate([here, below], 1)
        two_right = jnp.concatenate([pltpu.roll(here, LANES - XH, 1), pltpu.roll(below, LANES - XH, 1)], 1)
        edge = nt_dot(pair[...], jnp.concatenate([two, gap, two_right, gap], 0).astype(BF16))
        s = nn_dot(band[...], data)
        for z in range(ZB):
            for t in range(XT):
                value = s[XH * z + 8 * t : XH * z + 8 * t + 8]
                beyond = pltpu.roll(edge[8 * t : 8 * t + 8], YB - 1 - z, 1)
                sbuf[d, XH * z + 8 * t : XH * z + 8 * t + 8, :] = value + jnp.where(is_edge, beyond, pltpu.roll(value, LANES - 1, 1))

    def render(d, cum, bright, acc):
        for z in range(ZB):
            for t in range(XT):
                colour = lookup(sbuf[d, XH * z + 8 * t : XH * z + 8 * t + 8, :])
                inside = ent[8 * t : 8 * t + 8, :] <= ZB * d + z
                cum[t] = cum[t] + jnp.where(inside, colour[3], 0.0)
                bright_next = jnp.exp2(cum[t] * OPTICAL)
                weight = bright[t] - bright_next
                bright[t] = bright_next
                for c in range(3):
                    acc[c][t] = acc[c][t] + weight * colour[c]

    def fresh():
        for i in range(5 * XT):
            state[i] = one if XT <= i < 2 * XT else zero

    def two_bricks(i, _):
        d = (base + 2 * i) & (ND - 1)
        arrived(d + 1)

        @pl.when(i < ND // 2 - 1)
        def _():
            arrived((d + 2) & (ND - 1))

        @pl.when(d == 0)
        def _():
            behind[...] = state[...]
            fresh()

        sums(d)
        sums(d + 1)
        cum = [state[t] for t in range(XT)]
        bright = [state[XT + t] for t in range(XT)]
        acc = [[state[(2 + c) * XT + t] for t in range(XT)] for c in range(3)]
        render(d, cum, bright, acc)
        render(d + 1, cum, bright, acc)
        for i, v in enumerate(cum + bright + [v for a in acc for v in a]):
            state[i] = v
        return 0

    fresh()
    arrived(base)
    lax.fori_loop(0, ND // 2, two_bricks, 0)
    bright = [state[XT + t] * behind[XT + t] for t in range(XT)]
    acc = [
        [state[(2 + c) * XT + t] + state[XT + t] * behind[(2 + c) * XT + t] for t in range(XT)] for c in range(3)
    ]
    planes = jnp.concatenate([v * (UNIT * UNIT) for a in acc for v in a] + list(bright), 0)
    turned = planes.T
    for c in range(4):
        for h in range(2):
            out[c, :, XH * h : XH * (h + 1)] = turned[YB * h : YB * (h + 1), XH * c : XH * (c + 1)]

    early = pk.at[pl.ds(0, EARLY)]
    pltpu.make_async_copy(early, early, hsend).wait()
    rest = pk.at[pl.ds(0, ND - 1 - EARLY)]
    pltpu.make_async_copy(rest, rest, msend).wait()

    @pl.when(has_left)
    def _():
        pltpu.make_async_copy(ck, ck, csend).wait()


def shards(volume, entry_depth, tf_table):
    dma = pltpu.SemaphoreType.DMA
    return pl.pallas_call(
        kernel,
        out_shape=jax.ShapeDtypeStruct((4, YB, XB), F32),
        in_specs=[
            pl.BlockSpec(memory_space=pl.ANY),
            pl.BlockSpec(memory_space=pl.ANY),
            pl.BlockSpec(memory_space=pltpu.VMEM),
        ],
        out_specs=pl.BlockSpec(memory_space=pltpu.VMEM),
        scratch_shapes=[
            pltpu.VMEM((ZB, XB, NY), BF16),
            pltpu.VMEM((XB, LANES), I32),
            pltpu.VMEM((ND, ROWS, LANES), BF16),
            pltpu.VMEM((ND, TILE, LANES), BF16),
            pltpu.VMEM((ND + 1, ROWS, LANES), BF16),
            pltpu.VMEM((ND + 1, TILE, LANES), BF16),
            pltpu.VMEM((8, 8, LANES), I32),
            pltpu.VMEM((XH, LANES), I32),
            pltpu.VMEM((BODY, KROWS), BF16),
            pltpu.VMEM((XH, 2 * LANES), BF16),
            pltpu.VMEM((5 * XT, 8, LANES), F32),
            pltpu.VMEM((5 * XT, 8, LANES), F32),
            pltpu.VMEM((ND, BODY, LANES), F32),
            dma, dma, dma, dma, dma,
            dma((ND,)), dma((ND,)),
        ],
        compiler_params=pltpu.CompilerParams(collective_id=0, has_side_effects=True),
        name="render",
    )(volume, entry_depth, tf_table.T)


def solution(mesh):
    placed = (P("depth", "img", None), P("img", None), P())
    return jax.shard_map(
        shards, mesh=mesh, in_specs=placed, out_specs=P(None, "depth", "img"), check_vma=False
    )
```

time: 26.3 us -> 23.1 us (0.88)
  the two profiles are of different devices: /device:TPU:1 before, /device:TPU:102 now
where the time goes in v3:
time: 23.1 us; the launch traced here: 22.9 us
  Pallas kernels  21.3 us (92%)
  local copies, waits for them, and re-layouts  1.57 us (7%)
    pallas_call x1, Pallas kernels, shards(): pl.pallas_call(kernel, out_shape=jax.ShapeDtypeStruct((4, YB, XB), F32),...  21.3 us
    unnamed x1, local copies, waits for them, and re-layouts  1.57 us

profile of v3, /device:TPU:102, one launch (start us, length us, event | category | flops | bytes accessed | tf_op | source)
XLA Modules:
  0.0 22.9 jit_solution(9214760279434898932)
XLA Ops:
  0.0 21.3 %render.1 = f32[4,64,64]{2,1,0:T(8,128)} custom-call(bf16[4,64,1024]{2,1,0:T(8,128)(2,1)} %vol.1, s32[64,1024]{1,0:T(8,128)} %entry.1, f32[4,256]{1,0:T(4,128)} %bitcast.1), custom_call_target="tpu_custom_call" | custom-call | tf_op jit(solution)/shard_map/render/pallas_call | solution.py:325
  21.3 1.6 %copy.5 = f32[4,64,64]{2,1,0:T(8,128)} copy(f32[4,64,64]{2,1,0:T(8,128)} %render.1) | data formatting | bytes 131072

commit v4 on v3

v4 whole, which is shorter than its diff:
```python
import math

import jax
import jax.numpy as jnp
from jax import lax
from jax.experimental import pallas as pl
from jax.experimental.pallas import tpu as pltpu
from jax.sharding import PartitionSpec as P

MESH = pl.DeviceIdType.MESH
F32, BF16, I32 = jnp.float32, jnp.bfloat16, jnp.int32
ND = 16
NI = 16
ZB = 4
NZ = ND * ZB
XB = 64
XH = 32
XT = 8
NC = XH // XT
YB = 64
NY = ND * YB
LANES = 128
TILE = 8
CHUNK = ZB * XT
GROUP = 8
DEPTH = GROUP * XT + 2 * XT
SCALE = 255.0 / 8.0
UNIT = 2.0 / 65535.0
OPTICAL = -2.0 / NZ * math.log2(math.e) * UNIT * UNIT
PLANES = 32


def iota(shape, axis):
    return lax.broadcasted_iota(I32, shape, axis)


def choose(mask, value=1.0):
    return jnp.where(mask, value, 0.0).astype(BF16)


def nt_dot(a, b):
    return lax.dot_general(a, b, (((1,), (1,)), ((), ())), preferred_element_type=F32)


def nn_dot(a, b):
    return jnp.dot(a, b, preferred_element_type=F32)


def halves(a, b, low):
    turned = pltpu.roll(jnp.where(low, b, a), YB, 1)
    return jnp.where(low, a, turned), jnp.where(low, turned, b)


def band_matrix():
    row = iota((GROUP * XT, 2 * DEPTH), 0)
    col = iota((GROUP * XT, 2 * DEPTH), 1)
    second = col >= DEPTH
    local = jnp.where(second, col - DEPTH, col)
    dz = local // XT - row // XT
    dx = jnp.where(second, XT, 0) + local % XT - row % XT
    return choose((dz >= 0) & (dz <= 1) & (dx >= 0) & (dx <= 1), SCALE)


def kernel(
    vol, entry, table, out,
    vbuf, ebuf, pk, hk, ck, rb, hb, cb, hcb, words, ent, band, edges, sbuf, result,
    vsem, esem, bsend, hsend, csend, brecv, hrecv, crecv,
):
    me = lax.axis_index("depth")
    im = lax.axis_index("img")
    left = jnp.maximum(im - 1, 0)
    right = jnp.minimum(im + 1, NI - 1)
    has_left, has_right = im > 0, im < NI - 1

    def load(part, first):
        rows = pl.ds(first, 2 * XT)
        return pltpu.make_async_copy(vol.at[:, rows, :], vbuf.at[:, rows, :], vsem.at[part])

    firsts = (2 * XT, XH + 2 * XT, 0, XH)
    for part, first in enumerate(firsts):
        load(part, first).start()
    group = pl.multiple_of((me // 2) * LANES, LANES)
    load_entry = pltpu.make_async_copy(entry.at[:, pl.ds(group, LANES)], ebuf, esem)
    load_entry.start()

    barrier = pltpu.get_barrier_semaphore()
    for k in range(1, ND):
        pl.semaphore_signal(barrier, 1, device_id={"img": im, "depth": me ^ k}, device_id_type=MESH)

    @pl.when(has_right)
    def _():
        for k in range(ND):
            pl.semaphore_signal(barrier, 1, device_id={"img": right, "depth": me ^ k}, device_id_type=MESH)

    low = iota((2 * XT, LANES), 1) < YB
    low8 = iota((TILE, LANES), 1) < YB

    def pack(first_chunk):
        x = XT * first_chunk
        for g in range(ND // 2):
            lanes = slice(LANES * g, LANES * (g + 1))
            for z in range(ZB):
                pair = halves(vbuf[z, x : x + 2 * XT, lanes], vbuf[z, XH + x : XH + x + 2 * XT, lanes], low)
                for odd, v in enumerate(pair):
                    for c in range(2):
                        pk[(first_chunk + c) * ND + 2 * g + odd, XT * z : XT * (z + 1), :] = v[XT * c : XT * (c + 1)]

    def send_chunk(c):
        here = pl.ds(pl.multiple_of(CHUNK * me, CHUNK), CHUNK)
        for k in range(1, ND):
            pltpu.make_async_remote_copy(
                pk.at[c * ND + (me ^ k)], rb.at[c, here, :], bsend, brecv.at[c],
                device_id={"img": im, "depth": me ^ k}, device_id_type=MESH,
            ).start()
        pltpu.make_async_copy(pk.at[c * ND + me], rb.at[c, here, :], brecv.at[c]).start()

    load(0, firsts[0]).wait()
    load(1, firsts[1]).wait()
    pack(2)
    pl.semaphore_wait(barrier, jnp.where(has_left, 2 * ND - 1, ND - 1))
    send_chunk(3)

    load(2, firsts[2]).wait()
    load(3, firsts[3]).wait()
    sel = choose(iota((ND, NY), 1) == iota((ND, NY), 0) * YB + YB)
    zero_row = jnp.zeros((1, NY), F32)
    pad = jnp.zeros((ND, LANES - XB), F32)
    by_row = [jnp.concatenate([nt_dot(sel, vbuf[z]), pad], 1) for z in range(ZB)]
    first = jnp.concatenate([vbuf[z, 0:1, :].astype(F32) for z in range(ZB)] + [zero_row] * 4, 0)
    corner = nt_dot(sel, first.astype(BF16)).astype(BF16)
    spot = iota((LANES, ZB * ND), 0)
    block = iota((LANES, ZB * ND), 1)
    place = choose((spot // TILE == block % ND) & (spot % TILE == block // ND))
    mine = nn_dot(place, jnp.concatenate(by_row, 0).astype(BF16))
    spot16 = iota((LANES, ND), 0)
    spread = nn_dot(choose(spot16 // TILE == iota((LANES, ND), 1)), corner)
    lane8 = iota((LANES, TILE), 1)
    spread = jnp.sum(jnp.where(lane8 == iota((LANES, TILE), 0) % TILE, spread, 0.0), 1, keepdims=True)
    lane = iota((LANES, LANES), 1)
    at_corner = jnp.where((lane == YB) & (iota((LANES, LANES), 0) % TILE < ZB), jnp.broadcast_to(spread, (LANES, LANES)), 0.0)
    middle = jnp.concatenate([zero_row] * 4 + [vbuf[z, XH : XH + 1, :].astype(F32) for z in range(ZB)], 0)
    first = jnp.concatenate([zero_row] * 4 + [vbuf[z, 0:1, :].astype(F32) for z in range(ZB)], 0)
    for g in range(ND // 2):
        lanes = slice(LANES * g, LANES * (g + 1))
        a, b = middle[:, lanes], first[:, lanes]
        turned = pltpu.roll(jnp.where(low8, b, a), YB, 1)
        at = 2 * TILE * g
        hk[2 * g] = (mine[at : at + TILE] + jnp.where(low8, a, 0.0)).astype(BF16)
        hk[2 * g + 1] = (mine[at + TILE : at + 2 * TILE] + jnp.where(low8, turned, 0.0)).astype(BF16)
        ck[2 * g] = (at_corner[at : at + TILE] + jnp.where(low8, 0.0, turned)).astype(BF16)
        ck[2 * g + 1] = (at_corner[at + TILE : at + 2 * TILE] + jnp.where(low8, 0.0, b)).astype(BF16)

    tile_here = pl.ds(pl.multiple_of(TILE * me, TILE), TILE)
    for k in range(1, ND):
        pltpu.make_async_remote_copy(
            hk.at[me ^ k], hb.at[tile_here, :], hsend, hrecv,
            device_id={"img": im, "depth": me ^ k}, device_id_type=MESH,
        ).start()
    pltpu.make_async_copy(hk.at[me], hb.at[tile_here, :], hrecv).start()

    @pl.when(has_left)
    def _():
        for k in range(ND):
            pltpu.make_async_remote_copy(
                ck.at[me ^ k], cb.at[tile_here, :], csend, crecv,
                device_id={"img": left, "depth": me ^ k}, device_id_type=MESH,
            ).start()

    send_chunk(2)
    pack(0)
    send_chunk(1)
    send_chunk(0)

    for c in range(NC + 1):
        rb[c, ND * CHUNK : (ND + 1) * CHUNK, :] = jnp.zeros((CHUNK, LANES), BF16)

    @pl.when(jnp.logical_not(has_right))
    def _():
        cb[...] = jnp.zeros((ND * TILE, LANES), BF16)

    code = jnp.floor(jnp.sqrt(table[...]) * (1.0 / UNIT) + 0.5)
    code = jnp.concatenate([code, code], 0).astype(I32)
    lane128 = iota((8, LANES), 1)
    even_of = (2 * lane128) & (LANES - 1)

    def every_other(offset):
        lo, hi = (
            jnp.take_along_axis(part, even_of + offset, axis=1, mode="promise_in_bounds")
            for part in (code[:, :LANES], code[:, LANES:])
        )
        return jnp.where(lane128 < LANES // 2, lo, hi)

    even_code, odd_code = every_other(0), every_other(1)
    next_code = pltpu.roll(even_code, LANES - 1, 1)
    for c in range(4):
        words[c] = jnp.broadcast_to((even_code | (odd_code << 16))[c : c + 1], (8, LANES))
    for p in range(2):
        word = next_code[2 * p : 2 * p + 1] | (next_code[2 * p + 1 : 2 * p + 2] << 16)
        words[4 + p] = jnp.broadcast_to(word, (8, LANES))

    band[...] = band_matrix()

    load_entry.wait()
    low32 = iota((XH, LANES), 1) < YB
    even, odd = halves(ebuf[0:XH, :], ebuf[XH:XB, :], low32)
    ent[...] = jnp.where(lax.rem(me, 2) == 0, even, odd)

    is_edge = (iota((8, LANES), 1) & (YB - 1)) == YB - 1
    zero = jnp.zeros((8, LANES), F32)
    one = jnp.ones((8, LANES), F32)

    def make_edges(tiles):
        x = iota((XB, LANES), 0)
        dx = iota((XB, LANES), 1) - x
        sums = nt_dot(choose((dx >= 0) & (dx <= 1), SCALE), tiles)
        lane = iota((XB, LANES), 1)
        after = jnp.where(
            lane % TILE == ZB - 1,
            jnp.where(lane >= LANES - TILE, 0.0, pltpu.roll(sums, LANES - TILE + ZB - 1, 1)),
            pltpu.roll(sums, LANES - 1, 1),
        )
        sums += after
        front, back = halves(sums[:XH], sums[XH:], low32)
        edges[0] = front
        edges[1] = back

    def lookup(scaled):
        lower = jnp.minimum(jnp.floor(scaled), 254.0)
        frac = scaled - lower
        index = lower.astype(I32)
        odd = (index & 1) == 1
        within = lax.shift_right_logical(index, jnp.full_like(index, 1))

        def get(i):
            return jnp.take_along_axis(words[i], within, axis=1, mode="promise_in_bounds")

        values = []
        beyond = (get(4), get(5))
        for c in range(4):
            word = get(c)
            a = word & 65535
            b = lax.shift_right_logical(word, jnp.full_like(word, 16))
            e = beyond[c // 2]
            e = lax.shift_right_logical(e, jnp.full_like(e, 16)) if c % 2 else e & 65535
            lo = jnp.where(odd, b, a).astype(F32)
            hi = jnp.where(odd, e, b).astype(F32)
            lo = lo * lo
            hi = hi * hi
            values.append(lo + frac * (hi - lo))
        return values

    def wait_chunk(c):
        here = rb.at[c, pl.ds(0, ND * CHUNK), :]
        pltpu.make_async_copy(here, here, brecv.at[c]).wait()

    def column_tile(o, _):
        t = jnp.where(o == 0, 2, jnp.where(o == 1, 1, jnp.where(o == 2, 3, 0)))

        @pl.when(o == 0)
        def _():
            wait_chunk(3)
            wait_chunk(2)
            pltpu.make_async_copy(hb, hb, hrecv).wait()
            make_edges(hb[...])

        @pl.when(o == 1)
        def _():
            wait_chunk(1)

        @pl.when(o == 2)
        def _():
            @pl.when(has_right)
            def _():
                pltpu.make_async_copy(cb, cb, crecv).wait()

            hcb[...] = (hb[...].astype(F32) + cb[...].astype(F32)).astype(BF16)
            make_edges(hcb[...])
            n = ND // 2
            row = iota((n * CHUNK, n * TILE), 0)
            src = iota((n * CHUNK, n * TILE), 1)
            grow = choose((row // CHUNK == src // TILE) & (row % XT == 0) & (src % TILE == ZB + row // XT % ZB))
            for p in range(2):
                rows = nn_dot(grow, hcb[p * n * TILE : (p + 1) * n * TILE, :])
                rb[NC, p * n * CHUNK : (p + 1) * n * CHUNK, :] = rows.astype(BF16)

        @pl.when(o == 3)
        def _():
            wait_chunk(0)

        cols = pl.ds(pl.multiple_of(XT * t, XT), XT)
        for g in range(NZ // GROUP):
            at = GROUP * XT * g
            data = jnp.concatenate([rb[t, at : at + DEPTH, :], rb[t + 1, at : at + DEPTH, :]], 0)
            s = nn_dot(band[...], data)
            for z in range(GROUP):
                plane = GROUP * g + z
                d, r = plane // ZB, plane % ZB
                value = s[XT * z : XT * (z + 1)]
                beyond = pltpu.roll(edges[d // 8, cols, :], (YB - 1 - TILE * (d % 8) - r) % LANES, 1)
                sbuf[plane] = value + jnp.where(is_edge, beyond, pltpu.roll(value, LANES - 1, 1))

        entry_here = ent[cols, :]

        def planes(i, carry):
            cum, bright, acc = carry
            acc = list(acc)
            for p in range(PLANES):
                plane = PLANES * i + p
                colour = lookup(sbuf[plane])
                cum = cum + jnp.where(entry_here <= plane, colour[3], 0.0)
                bright_next = jnp.exp2(cum * OPTICAL)
                weight = bright - bright_next
                bright = bright_next
                for c in range(3):
                    acc[c] = acc[c] + weight * colour[c]
            return cum, bright, tuple(acc)

        _, bright, acc = lax.fori_loop(0, NZ // PLANES, planes, (zero, one, (zero,) * 3))
        for c in range(3):
            result[c, cols, :] = acc[c] * (UNIT * UNIT)
        result[3, cols, :] = bright
        return 0

    lax.fori_loop(0, NC, column_tile, 0)
    turned = result[...].reshape(4 * XH, LANES).T
    for c in range(4):
        for h in range(2):
            out[c, :, XH * h : XH * (h + 1)] = turned[YB * h : YB * (h + 1), XH * c : XH * (c + 1)]

    sent = pk.at[pl.ds(0, NC * (ND - 1))]
    pltpu.make_async_copy(sent, sent, bsend).wait()
    tiles = hk.at[pl.ds(0, ND - 1)]
    pltpu.make_async_copy(tiles, tiles, hsend).wait()

    @pl.when(has_left)
    def _():
        pltpu.make_async_copy(ck, ck, csend).wait()


def shards(volume, entry_depth, tf_table):
    dma = pltpu.SemaphoreType.DMA
    return pl.pallas_call(
        kernel,
        out_shape=jax.ShapeDtypeStruct((4, YB, XB), F32),
        in_specs=[
            pl.BlockSpec(memory_space=pl.ANY),
            pl.BlockSpec(memory_space=pl.ANY),
            pl.BlockSpec(memory_space=pltpu.VMEM),
        ],
        out_specs=pl.BlockSpec(memory_space=pltpu.VMEM),
        scratch_shapes=[
            pltpu.VMEM((ZB, XB, NY), BF16),
            pltpu.VMEM((XB, LANES), I32),
            pltpu.VMEM((NC * ND, CHUNK, LANES), BF16),
            pltpu.VMEM((ND, TILE, LANES), BF16),
            pltpu.VMEM((ND, TILE, LANES), BF16),
            pltpu.VMEM((NC + 1, (ND + 1) * CHUNK, LANES), BF16),
            pltpu.VMEM((ND * TILE, LANES), BF16),
            pltpu.VMEM((ND * TILE, LANES), BF16),
            pltpu.VMEM((ND * TILE, LANES), BF16),
            pltpu.VMEM((6, 8, LANES), I32),
            pltpu.VMEM((XH, LANES), I32),
            pltpu.VMEM((GROUP * XT, 2 * DEPTH), BF16),
            pltpu.VMEM((2, XH, LANES), F32),
            pltpu.VMEM((NZ, XT, LANES), F32),
            pltpu.VMEM((4, XH, LANES), F32),
            dma((4,)), dma, dma, dma, dma,
            dma((NC,)), dma, dma,
        ],
        compiler_params=pltpu.CompilerParams(collective_id=0, has_side_effects=True),
        name="render",
    )(volume, entry_depth, tf_table.T)


def solution(mesh):
    placed = (P("depth", "img", None), P("img", None), P())
    return jax.shard_map(
        shards, mesh=mesh, in_specs=placed, out_specs=P(None, "depth", "img"), check_vma=False
    )
```

time: 23.1 us -> 21.5 us (0.931)
  the two profiles are of different devices: /device:TPU:102 before, /device:TPU:1 now
where the time goes in v4:
time: 21.5 us; the launch traced here: 21.4 us
  Pallas kernels  19.8 us (92%)
  local copies, waits for them, and re-layouts  1.57 us (7%)
    pallas_call x1, Pallas kernels, shards(): pl.pallas_call(kernel, out_shape=jax.ShapeDtypeStruct((4, YB, XB), F32),...  19.8 us
    unnamed x1, local copies, waits for them, and re-layouts  1.57 us

profile of v4, /device:TPU:1, one launch (start us, length us, event | category | flops | bytes accessed | tf_op | source)
XLA Modules:
  0.0 21.4 jit_solution(14057926152696189376)
XLA Ops:
  0.0 19.8 %render.1 = f32[4,64,64]{2,1,0:T(8,128)} custom-call(bf16[4,64,1024]{2,1,0:T(8,128)(2,1)} %vol.1, s32[64,1024]{1,0:T(8,128)} %entry.1, f32[4,256]{1,0:T(4,128)} %bitcast.1), custom_call_target="tpu_custom_call" | custom-call | tf_op jit(solution)/shard_map/render/pallas_call | solution.py:342
  19.8 1.6 %copy.5 = f32[4,64,64]{2,1,0:T(8,128)} copy(f32[4,64,64]{2,1,0:T(8,128)} %render.1) | data formatting | bytes 131072

commit v5 on v4

--- a/solution.py
+++ b/solution.py
@@ -28,6 +28,7 @@
 UNIT = 2.0 / 65535.0
 OPTICAL = -2.0 / NZ * math.log2(math.e) * UNIT * UNIT
 PLANES = 32
+FAR_FIRST = sorted(range(1, ND), key=lambda k: -((0, 1, 2, 1)[k & 3] + (0, 1, 2, 1)[k >> 2]))
 
 
 def iota(shape, axis):
@@ -64,7 +65,7 @@
 def kernel(
     vol, entry, table, out,
     vbuf, ebuf, pk, hk, ck, rb, hb, cb, hcb, words, ent, band, edges, sbuf, result,
-    vsem, esem, bsend, hsend, csend, brecv, hrecv, crecv,
+    vsem, esem, bsend, hsend, csend, brecv, hrecv, crecv, go,
 ):
     me = lax.axis_index("depth")
     im = lax.axis_index("img")
@@ -84,13 +85,12 @@
     load_entry.start()
 
     barrier = pltpu.get_barrier_semaphore()
-    for k in range(1, ND):
+    for k in FAR_FIRST:
         pl.semaphore_signal(barrier, 1, device_id={"img": im, "depth": me ^ k}, device_id_type=MESH)
 
-    @pl.when(has_right)
-    def _():
-        for k in range(ND):
-            pl.semaphore_signal(barrier, 1, device_id={"img": right, "depth": me ^ k}, device_id_type=MESH)
+    @pl.when(has_left)
+    def _():
+        pl.semaphore_signal(barrier, 1, device_id={"img": left, "depth": me}, device_id_type=MESH)
 
     low = iota((2 * XT, LANES), 1) < YB
     low8 = iota((TILE, LANES), 1) < YB
@@ -107,7 +107,7 @@
 
     def send_chunk(c):
         here = pl.ds(pl.multiple_of(CHUNK * me, CHUNK), CHUNK)
-        for k in range(1, ND):
+        for k in FAR_FIRST:
             pltpu.make_async_remote_copy(
                 pk.at[c * ND + (me ^ k)], rb.at[c, here, :], bsend, brecv.at[c],
                 device_id={"img": im, "depth": me ^ k}, device_id_type=MESH,
@@ -117,7 +117,12 @@
     load(0, firsts[0]).wait()
     load(1, firsts[1]).wait()
     pack(2)
-    pl.semaphore_wait(barrier, jnp.where(has_left, 2 * ND - 1, ND - 1))
+    pl.semaphore_wait(barrier, jnp.where(has_right, ND, ND - 1))
+
+    @pl.when(has_right)
+    def _():
+        pl.semaphore_signal(go, 1, device_id={"img": right, "depth": me}, device_id_type=MESH)
+
     send_chunk(3)
 
     load(2, firsts[2]).wait()
@@ -151,7 +156,7 @@
         ck[2 * g + 1] = (at_corner[at + TILE : at + 2 * TILE] + jnp.where(low8, 0.0, b)).astype(BF16)
 
     tile_here = pl.ds(pl.multiple_of(TILE * me, TILE), TILE)
-    for k in range(1, ND):
+    for k in FAR_FIRST:
         pltpu.make_async_remote_copy(
             hk.at[me ^ k], hb.at[tile_here, :], hsend, hrecv,
             device_id={"img": im, "depth": me ^ k}, device_id_type=MESH,
@@ -160,6 +165,7 @@
 
     @pl.when(has_left)
     def _():
+        pl.semaphore_wait(go, 1)
         for k in range(ND):
             pltpu.make_async_remote_copy(
                 ck.at[me ^ k], cb.at[tile_here, :], csend, crecv,
@@ -191,7 +197,7 @@
         return jnp.where(lane128 < LANES // 2, lo, hi)
 
     even_code, odd_code = every_other(0), every_other(1)
-    next_code = pltpu.roll(even_code, LANES - 1, 1)
+    next_code = jnp.where(lane128 == LANES - 1, odd_code, pltpu.roll(even_code, LANES - 1, 1))
     for c in range(4):
         words[c] = jnp.broadcast_to((even_code | (odd_code << 16))[c : c + 1], (8, LANES))
     for p in range(2):
@@ -221,11 +227,16 @@
         )
         sums += after
         front, back = halves(sums[:XH], sums[XH:], low32)
-        edges[0] = front
-        edges[1] = back
+        return front, back
+
+    def place_edges(t, front, back):
+        for plane in range(NZ):
+            d, r = plane // ZB, plane % ZB
+            at = (YB - 1 - TILE * (d % 8) - r) % LANES
+            edges[t, plane] = pltpu.roll((front, back)[d // 8][XT * t : XT * (t + 1)], at, 1)
 
     def lookup(scaled):
-        lower = jnp.minimum(jnp.floor(scaled), 254.0)
+        lower = jnp.floor(scaled)
         frac = scaled - lower
         index = lower.astype(I32)
         odd = (index & 1) == 1
@@ -254,27 +265,25 @@
         pltpu.make_async_copy(here, here, brecv.at[c]).wait()
 
     def column_tile(o, _):
-        t = jnp.where(o == 0, 2, jnp.where(o == 1, 1, jnp.where(o == 2, 3, 0)))
+        t = jnp.where(o == 0, 2, jnp.where(o == 1, 3, 3 - o))
 
         @pl.when(o == 0)
         def _():
+            pltpu.make_async_copy(hb, hb, hrecv).wait()
+            both = make_edges(hb[...])
+            for t in range(NC - 1):
+                place_edges(t, *both)
             wait_chunk(3)
             wait_chunk(2)
-            pltpu.make_async_copy(hb, hb, hrecv).wait()
-            make_edges(hb[...])
 
         @pl.when(o == 1)
-        def _():
-            wait_chunk(1)
-
-        @pl.when(o == 2)
         def _():
             @pl.when(has_right)
             def _():
                 pltpu.make_async_copy(cb, cb, crecv).wait()
 
             hcb[...] = (hb[...].astype(F32) + cb[...].astype(F32)).astype(BF16)
-            make_edges(hcb[...])
+            place_edges(NC - 1, *make_edges(hcb[...]))
             n = ND // 2
             row = iota((n * CHUNK, n * TILE), 0)
             src = iota((n * CHUNK, n * TILE), 1)
@@ -283,6 +292,10 @@
                 rows = nn_dot(grow, hcb[p * n * TILE : (p + 1) * n * TILE, :])
                 rb[NC, p * n * CHUNK : (p + 1) * n * CHUNK, :] = rows.astype(BF16)
 
+        @pl.when(o == 2)
+        def _():
+            wait_chunk(1)
+
         @pl.when(o == 3)
         def _():
             wait_chunk(0)
@@ -294,10 +307,8 @@
             s = nn_dot(band[...], data)
             for z in range(GROUP):
                 plane = GROUP * g + z
-                d, r = plane // ZB, plane % ZB
                 value = s[XT * z : XT * (z + 1)]
-                beyond = pltpu.roll(edges[d // 8, cols, :], (YB - 1 - TILE * (d % 8) - r) % LANES, 1)
-                sbuf[plane] = value + jnp.where(is_edge, beyond, pltpu.roll(value, LANES - 1, 1))
+                sbuf[plane] = value + jnp.where(is_edge, edges[t, plane], pltpu.roll(value, LANES - 1, 1))
 
         entry_here = ent[cols, :]
 
@@ -361,11 +372,11 @@
             pltpu.VMEM((6, 8, LANES), I32),
             pltpu.VMEM((XH, LANES), I32),
             pltpu.VMEM((GROUP * XT, 2 * DEPTH), BF16),
-            pltpu.VMEM((2, XH, LANES), F32),
+            pltpu.VMEM((NC, NZ, XT, LANES), F32),
             pltpu.VMEM((NZ, XT, LANES), F32),
             pltpu.VMEM((4, XH, LANES), F32),
             dma((4,)), dma, dma, dma, dma,
-            dma((NC,)), dma, dma,
+            dma((NC,)), dma, dma, pltpu.SemaphoreType.REGULAR,
         ],
         compiler_params=pltpu.CompilerParams(collective_id=0, has_side_effects=True),
         name="render",

time: 21.5 us -> 21.3 us (level)
  the two profiles are of different devices: /device:TPU:1 before, /device:TPU:97 now
where the time goes in v5:
time: 21.3 us; the launch traced here: 21.2 us
  Pallas kernels  19.6 us (92%)
  local copies, waits for them, and re-layouts  1.57 us (7%)
    pallas_call x1, Pallas kernels, shards(): pl.pallas_call(kernel, out_shape=jax.ShapeDtypeStruct((4, YB, XB), F32),...  19.6 us
    unnamed x1, local copies, waits for them, and re-layouts  1.57 us

profile of v5, /device:TPU:97, one launch (start us, length us, event | category | flops | bytes accessed | tf_op | source)
XLA Modules:
  0.0 21.2 jit_solution(5610710951346738297)
XLA Ops:
  0.0 19.6 %render.1 = f32[4,64,64]{2,1,0:T(8,128)} custom-call(bf16[4,64,1024]{2,1,0:T(8,128)(2,1)} %vol.1, s32[64,1024]{1,0:T(8,128)} %entry.1, f32[4,256]{1,0:T(4,128)} %bitcast.1), custom_call_target="tpu_custom_call" | custom-call | tf_op jit(solution)/shard_map/render/pallas_call | solution.py:353
  19.6 1.6 %copy.5 = f32[4,64,64]{2,1,0:T(8,128)} copy(f32[4,64,64]{2,1,0:T(8,128)} %render.1) | data formatting | bytes 131072

commit v6 on v5

--- a/solution.py
+++ b/solution.py
@@ -24,10 +24,10 @@
 CHUNK = ZB * XT
 GROUP = 8
 DEPTH = GROUP * XT + 2 * XT
-SCALE = 255.0 / 8.0
+SCALE = 255.0 / 16.0
 UNIT = 2.0 / 65535.0
 OPTICAL = -2.0 / NZ * math.log2(math.e) * UNIT * UNIT
-PLANES = 32
+PLANES = 64
 FAR_FIRST = sorted(range(1, ND), key=lambda k: -((0, 1, 2, 1)[k & 3] + (0, 1, 2, 1)[k >> 2]))
 
 
@@ -117,16 +117,9 @@
     load(0, firsts[0]).wait()
     load(1, firsts[1]).wait()
     pack(2)
-    pl.semaphore_wait(barrier, jnp.where(has_right, ND, ND - 1))
-
-    @pl.when(has_right)
-    def _():
-        pl.semaphore_signal(go, 1, device_id={"img": right, "depth": me}, device_id_type=MESH)
-
-    send_chunk(3)
-
     load(2, firsts[2]).wait()
     load(3, firsts[3]).wait()
+    pack(0)
     sel = choose(iota((ND, NY), 1) == iota((ND, NY), 0) * YB + YB)
     zero_row = jnp.zeros((1, NY), F32)
     pad = jnp.zeros((ND, LANES - XB), F32)
@@ -155,6 +148,12 @@
         ck[2 * g] = (at_corner[at : at + TILE] + jnp.where(low8, 0.0, turned)).astype(BF16)
         ck[2 * g + 1] = (at_corner[at + TILE : at + 2 * TILE] + jnp.where(low8, 0.0, b)).astype(BF16)
 
+    pl.semaphore_wait(barrier, jnp.where(has_right, ND, ND - 1))
+
+    @pl.when(has_right)
+    def _():
+        pl.semaphore_signal(go, 1, device_id={"img": right, "depth": me}, device_id_type=MESH)
+
     tile_here = pl.ds(pl.multiple_of(TILE * me, TILE), TILE)
     for k in FAR_FIRST:
         pltpu.make_async_remote_copy(
@@ -163,6 +162,9 @@
         ).start()
     pltpu.make_async_copy(hk.at[me], hb.at[tile_here, :], hrecv).start()
 
+    send_chunk(3)
+    send_chunk(2)
+
     @pl.when(has_left)
     def _():
         pl.semaphore_wait(go, 1)
@@ -172,8 +174,6 @@
                 device_id={"img": left, "depth": me ^ k}, device_id_type=MESH,
             ).start()
 
-    send_chunk(2)
-    pack(0)
     send_chunk(1)
     send_chunk(0)
 
@@ -199,7 +199,8 @@
     even_code, odd_code = every_other(0), every_other(1)
     next_code = jnp.where(lane128 == LANES - 1, odd_code, pltpu.roll(even_code, LANES - 1, 1))
     for c in range(4):
-        words[c] = jnp.broadcast_to((even_code | (odd_code << 16))[c : c + 1], (8, LANES))
+        word = (odd_code | (even_code << 16)) if c % 2 else (even_code | (odd_code << 16))
+        words[c] = jnp.broadcast_to(word[c : c + 1], (8, LANES))
     for p in range(2):
         word = next_code[2 * p : 2 * p + 1] | (next_code[2 * p + 1 : 2 * p + 2] << 16)
         words[4 + p] = jnp.broadcast_to(word, (8, LANES))
@@ -235,29 +236,31 @@
             at = (YB - 1 - TILE * (d % 8) - r) % LANES
             edges[t, plane] = pltpu.roll((front, back)[d // 8][XT * t : XT * (t + 1)], at, 1)
 
-    def lookup(scaled):
-        lower = jnp.floor(scaled)
-        frac = scaled - lower
-        index = lower.astype(I32)
-        odd = (index & 1) == 1
-        within = lax.shift_right_logical(index, jnp.full_like(index, 1))
+    def lookup(pairs):
+        pair = pairs.astype(I32)
+        r = pairs - pair.astype(F32)
+        beyond = r >= 0.5
+        away = jnp.abs(r + r - 1.0)
 
         def get(i):
-            return jnp.take_along_axis(words[i], within, axis=1, mode="promise_in_bounds")
+            return jnp.take_along_axis(words[i], pair, axis=1, mode="promise_in_bounds")
+
+        def upper(v):
+            return lax.shift_right_logical(v, jnp.full_like(v, 16))
+
+        def lower(v):
+            return v & 65535
 
         values = []
-        beyond = (get(4), get(5))
+        after = (get(4), get(5))
         for c in range(4):
             word = get(c)
-            a = word & 65535
-            b = lax.shift_right_logical(word, jnp.full_like(word, 16))
-            e = beyond[c // 2]
-            e = lax.shift_right_logical(e, jnp.full_like(e, 16)) if c % 2 else e & 65535
-            lo = jnp.where(odd, b, a).astype(F32)
-            hi = jnp.where(odd, e, b).astype(F32)
-            lo = lo * lo
-            hi = hi * hi
-            values.append(lo + frac * (hi - lo))
+            x = jnp.where(beyond, after[c // 2], word)
+            x, b = (upper(x), lower(word)) if c % 2 else (lower(x), upper(word))
+            x, b = x.astype(F32), b.astype(F32)
+            x = x * x
+            b = b * b
+            values.append(b + away * (x - b))
         return values
 
     def wait_chunk(c):

time: 21.3 us -> 20.4 us (0.958)
  Pallas kernels: 19.6 us -> 18.6 us
    pallas_call x1, Pallas kernels: 19.6 us -> 18.6 us  [shards(): pl.pallas_call(kernel, out_shape=jax.ShapeDtypeStruct((4, YB, XB), F32),...]
where the time goes in v6:
time: 20.4 us; the launch traced here: 20.2 us
  Pallas kernels  18.6 us (91%)
  local copies, waits for them, and re-layouts  1.57 us (8%)
    pallas_call x1, Pallas kernels, shards(): pl.pallas_call(kernel, out_shape=jax.ShapeDtypeStruct((4, YB, XB), F32),...  18.6 us
    unnamed x1, local copies, waits for them, and re-layouts  1.57 us

profile of v6, /device:TPU:97, one launch (start us, length us, event | category | flops | bytes accessed | tf_op | source)
XLA Modules:
  0.0 20.2 jit_solution(14446684911358697501)
XLA Ops:
  0.0 18.6 %render.1 = f32[4,64,64]{2,1,0:T(8,128)} custom-call(bf16[4,64,1024]{2,1,0:T(8,128)(2,1)} %vol.1, s32[64,1024]{1,0:T(8,128)} %entry.1, f32[4,256]{1,0:T(4,128)} %bitcast.1), custom_call_target="tpu_custom_call" | custom-call | tf_op jit(solution)/shard_map/render/pallas_call | solution.py:356
  18.6 1.6 %copy.5 = f32[4,64,64]{2,1,0:T(8,128)} copy(f32[4,64,64]{2,1,0:T(8,128)} %render.1) | data formatting | bytes 131072

commit v7 on v6

--- a/solution.py
+++ b/solution.py
@@ -24,6 +24,7 @@
 CHUNK = ZB * XT
 GROUP = 8
 DEPTH = GROUP * XT + 2 * XT
+SIDE = 4 * TILE
 SCALE = 255.0 / 16.0
 UNIT = 2.0 / 65535.0
 OPTICAL = -2.0 / NZ * math.log2(math.e) * UNIT * UNIT
@@ -62,10 +63,21 @@
     return choose((dz >= 0) & (dz <= 1) & (dx >= 0) & (dx <= 1), SCALE)
 
 
+def side_matrix():
+    row = iota((GROUP * XT, DEPTH + SIDE), 0)
+    col = iota((GROUP * XT, DEPTH + SIDE), 1)
+    tile = col - DEPTH
+    second = tile >= 0
+    dz = jnp.where(second, tile // TILE * ZB + tile % TILE - ZB, col // XT) - row // XT
+    dx = jnp.where(second, XT, col % XT) - row % XT
+    used = (tile < 0) | (tile % TILE >= ZB)
+    return choose(used & (dz >= 0) & (dz <= 1) & (dx >= 0) & (dx <= 1), SCALE)
+
+
 def kernel(
     vol, entry, table, out,
-    vbuf, ebuf, pk, hk, ck, rb, hb, cb, hcb, words, ent, band, edges, sbuf, result,
-    vsem, esem, bsend, hsend, csend, brecv, hrecv, crecv, go,
+    vbuf, ebuf, tbuf, pk, hk, ck, rb, hb, cb, hcb, words, ent, band, side_band, pair, edges, sbuf, result,
+    vsem, esem, tsem, bsend, hsend, csend, brecv, hrecv, crecv, go,
 ):
     me = lax.axis_index("depth")
     im = lax.axis_index("img")
@@ -83,6 +95,8 @@
     group = pl.multiple_of((me // 2) * LANES, LANES)
     load_entry = pltpu.make_async_copy(entry.at[:, pl.ds(group, LANES)], ebuf, esem)
     load_entry.start()
+    load_table = pltpu.make_async_copy(table, tbuf, tsem)
+    load_table.start()
 
     barrier = pltpu.get_barrier_semaphore()
     for k in FAR_FIRST:
@@ -148,6 +162,41 @@
         ck[2 * g] = (at_corner[at : at + TILE] + jnp.where(low8, 0.0, turned)).astype(BF16)
         ck[2 * g + 1] = (at_corner[at + TILE : at + 2 * TILE] + jnp.where(low8, 0.0, b)).astype(BF16)
 
+    hcb[ND * TILE : (ND + 2) * TILE, :] = jnp.zeros((2 * TILE, LANES), BF16)
+    for c in range(NC):
+        rb[c, ND * CHUNK : (ND + 1) * CHUNK, :] = jnp.zeros((CHUNK, LANES), BF16)
+
+    @pl.when(jnp.logical_not(has_right))
+    def _():
+        cb[...] = jnp.zeros((ND * TILE, LANES), BF16)
+
+    load_table.wait()
+    code = jnp.floor(jnp.sqrt(tbuf[...]) * (1.0 / UNIT) + 0.5)
+    code = jnp.concatenate([code, code], 0).astype(I32)
+    lane128 = iota((8, LANES), 1)
+    even_of = (2 * lane128) & (LANES - 1)
+
+    def every_other(offset):
+        lo, hi = (
+            jnp.take_along_axis(part, even_of + offset, axis=1, mode="promise_in_bounds")
+            for part in (code[:, :LANES], code[:, LANES:])
+        )
+        return jnp.where(lane128 < LANES // 2, lo, hi)
+
+    even_code, odd_code = every_other(0), every_other(1)
+    next_code = jnp.where(lane128 == LANES - 1, odd_code, pltpu.roll(even_code, LANES - 1, 1))
+    for c in range(4):
+        word = (odd_code | (even_code << 16)) if c % 2 else (even_code | (odd_code << 16))
+        words[c] = jnp.broadcast_to(word[c : c + 1], (8, LANES))
+    for p in range(2):
+        word = next_code[2 * p : 2 * p + 1] | (next_code[2 * p + 1 : 2 * p + 2] << 16)
+        words[4 + p] = jnp.broadcast_to(word, (8, LANES))
+
+    band[...] = band_matrix()
+    side_band[...] = side_matrix()
+    dx = iota((XB, LANES), 1) - iota((XB, LANES), 0)
+    pair[...] = choose((dx >= 0) & (dx <= 1), SCALE)
+
     pl.semaphore_wait(barrier, jnp.where(has_right, ND, ND - 1))
 
     @pl.when(has_right)
@@ -177,36 +226,6 @@
     send_chunk(1)
     send_chunk(0)
 
-    for c in range(NC + 1):
-        rb[c, ND * CHUNK : (ND + 1) * CHUNK, :] = jnp.zeros((CHUNK, LANES), BF16)
-
-    @pl.when(jnp.logical_not(has_right))
-    def _():
-        cb[...] = jnp.zeros((ND * TILE, LANES), BF16)
-
-    code = jnp.floor(jnp.sqrt(table[...]) * (1.0 / UNIT) + 0.5)
-    code = jnp.concatenate([code, code], 0).astype(I32)
-    lane128 = iota((8, LANES), 1)
-    even_of = (2 * lane128) & (LANES - 1)
-
-    def every_other(offset):
-        lo, hi = (
-            jnp.take_along_axis(part, even_of + offset, axis=1, mode="promise_in_bounds")
-            for part in (code[:, :LANES], code[:, LANES:])
-        )
-        return jnp.where(lane128 < LANES // 2, lo, hi)
-
-    even_code, odd_code = every_other(0), every_other(1)
-    next_code = jnp.where(lane128 == LANES - 1, odd_code, pltpu.roll(even_code, LANES - 1, 1))
-    for c in range(4):
-        word = (odd_code | (even_code << 16)) if c % 2 else (even_code | (odd_code << 16))
-        words[c] = jnp.broadcast_to(word[c : c + 1], (8, LANES))
-    for p in range(2):
-        word = next_code[2 * p : 2 * p + 1] | (next_code[2 * p + 1 : 2 * p + 2] << 16)
-        words[4 + p] = jnp.broadcast_to(word, (8, LANES))
-
-    band[...] = band_matrix()
-
     load_entry.wait()
     low32 = iota((XH, LANES), 1) < YB
     even, odd = halves(ebuf[0:XH, :], ebuf[XH:XB, :], low32)
@@ -216,25 +235,23 @@
     zero = jnp.zeros((8, LANES), F32)
     one = jnp.ones((8, LANES), F32)
 
-    def make_edges(tiles):
-        x = iota((XB, LANES), 0)
-        dx = iota((XB, LANES), 1) - x
-        sums = nt_dot(choose((dx >= 0) & (dx <= 1), SCALE), tiles)
-        lane = iota((XB, LANES), 1)
+    def make_edges(left_rows, right_rows, tiles, is_low):
+        n = left_rows.shape[0]
+        sums = nt_dot(jnp.concatenate([left_rows, right_rows], 0), tiles)
+        lane = iota((2 * n, LANES), 1)
         after = jnp.where(
             lane % TILE == ZB - 1,
             jnp.where(lane >= LANES - TILE, 0.0, pltpu.roll(sums, LANES - TILE + ZB - 1, 1)),
             pltpu.roll(sums, LANES - 1, 1),
         )
         sums += after
-        front, back = halves(sums[:XH], sums[XH:], low32)
-        return front, back
+        return halves(sums[:n], sums[n:], is_low)
 
     def place_edges(t, front, back):
         for plane in range(NZ):
             d, r = plane // ZB, plane % ZB
             at = (YB - 1 - TILE * (d % 8) - r) % LANES
-            edges[t, plane] = pltpu.roll((front, back)[d // 8][XT * t : XT * (t + 1)], at, 1)
+            edges[t, plane] = pltpu.roll((front, back)[d // 8], at, 1)
 
     def lookup(pairs):
         pair = pairs.astype(I32)
@@ -267,15 +284,21 @@
         here = rb.at[c, pl.ds(0, ND * CHUNK), :]
         pltpu.make_async_copy(here, here, brecv.at[c]).wait()
 
+    def store_sums(g, t, s):
+        for z in range(GROUP):
+            plane = GROUP * g + z
+            value = s[XT * z : XT * (z + 1)]
+            sbuf[plane] = value + jnp.where(is_edge, edges[t, plane], pltpu.roll(value, LANES - 1, 1))
+
     def column_tile(o, _):
         t = jnp.where(o == 0, 2, jnp.where(o == 1, 3, 3 - o))
 
         @pl.when(o == 0)
         def _():
             pltpu.make_async_copy(hb, hb, hrecv).wait()
-            both = make_edges(hb[...])
+            front, back = make_edges(pair[0:XH, :], pair[XH:XB, :], hb[...], low32)
             for t in range(NC - 1):
-                place_edges(t, *both)
+                place_edges(t, front[XT * t : XT * (t + 1)], back[XT * t : XT * (t + 1)])
             wait_chunk(3)
             wait_chunk(2)
 
@@ -285,15 +308,12 @@
             def _():
                 pltpu.make_async_copy(cb, cb, crecv).wait()
 
-            hcb[...] = (hb[...].astype(F32) + cb[...].astype(F32)).astype(BF16)
-            place_edges(NC - 1, *make_edges(hcb[...]))
-            n = ND // 2
-            row = iota((n * CHUNK, n * TILE), 0)
-            src = iota((n * CHUNK, n * TILE), 1)
-            grow = choose((row // CHUNK == src // TILE) & (row % XT == 0) & (src % TILE == ZB + row // XT % ZB))
-            for p in range(2):
-                rows = nn_dot(grow, hcb[p * n * TILE : (p + 1) * n * TILE, :])
-                rb[NC, p * n * CHUNK : (p + 1) * n * CHUNK, :] = rows.astype(BF16)
+            hcb[0 : ND * TILE, :] = (hb[...].astype(F32) + cb[...].astype(F32)).astype(BF16)
+            place_edges(NC - 1, *make_edges(pair[XH - XT : XH, :], pair[XB - XT : XB, :], hcb[0 : ND * TILE, :], low8))
+            for g in range(NZ // GROUP):
+                at = GROUP * XT * g
+                tiles = hcb[2 * TILE * g : 2 * TILE * g + SIDE, :]
+                store_sums(g, NC - 1, nn_dot(side_band[...], jnp.concatenate([rb[NC - 1, at : at + DEPTH, :], tiles], 0)))
 
         @pl.when(o == 2)
         def _():
@@ -304,14 +324,12 @@
             wait_chunk(0)
 
         cols = pl.ds(pl.multiple_of(XT * t, XT), XT)
-        for g in range(NZ // GROUP):
-            at = GROUP * XT * g
-            data = jnp.concatenate([rb[t, at : at + DEPTH, :], rb[t + 1, at : at + DEPTH, :]], 0)
-            s = nn_dot(band[...], data)
-            for z in range(GROUP):
-                plane = GROUP * g + z
-                value = s[XT * z : XT * (z + 1)]
-                sbuf[plane] = value + jnp.where(is_edge, edges[t, plane], pltpu.roll(value, LANES - 1, 1))
+        @pl.when(o != 1)
+        def _():
+            for g in range(NZ // GROUP):
+                at = GROUP * XT * g
+                data = jnp.concatenate([rb[t, at : at + DEPTH, :], rb[t + 1, at : at + DEPTH, :]], 0)
+                store_sums(g, t, nn_dot(band[...], data))
 
         entry_here = ent[cols, :]
 
@@ -359,26 +377,29 @@
         in_specs=[
             pl.BlockSpec(memory_space=pl.ANY),
             pl.BlockSpec(memory_space=pl.ANY),
-            pl.BlockSpec(memory_space=pltpu.VMEM),
+            pl.BlockSpec(memory_space=pl.ANY),
         ],
         out_specs=pl.BlockSpec(memory_space=pltpu.VMEM),
         scratch_shapes=[
             pltpu.VMEM((ZB, XB, NY), BF16),
             pltpu.VMEM((XB, LANES), I32),
+            pltpu.VMEM((4, 2 * LANES), F32),
             pltpu.VMEM((NC * ND, CHUNK, LANES), BF16),
             pltpu.VMEM((ND, TILE, LANES), BF16),
             pltpu.VMEM((ND, TILE, LANES), BF16),
-            pltpu.VMEM((NC + 1, (ND + 1) * CHUNK, LANES), BF16),
+            pltpu.VMEM((NC, (ND + 1) * CHUNK, LANES), BF16),
             pltpu.VMEM((ND * TILE, LANES), BF16),
             pltpu.VMEM((ND * TILE, LANES), BF16),
-            pltpu.VMEM((ND * TILE, LANES), BF16),
+            pltpu.VMEM(((ND + 2) * TILE, LANES), BF16),
             pltpu.VMEM((6, 8, LANES), I32),
             pltpu.VMEM((XH, LANES), I32),
             pltpu.VMEM((GROUP * XT, 2 * DEPTH), BF16),
+            pltpu.VMEM((GROUP * XT, DEPTH + SIDE), BF16),
+            pltpu.VMEM((XB, LANES), BF16),
             pltpu.VMEM((NC, NZ, XT, LANES), F32),
             pltpu.VMEM((NZ, XT, LANES), F32),
             pltpu.VMEM((4, XH, LANES), F32),
-            dma((4,)), dma, dma, dma, dma,
+            dma((4,)), dma, dma, dma, dma, dma,
             dma((NC,)), dma, dma, pltpu.SemaphoreType.REGULAR,
         ],
         compiler_params=pltpu.CompilerParams(collective_id=0, has_side_effects=True),

time: 20.4 us -> 19.4 us (0.951)
  Pallas kernels: 18.6 us -> 17.7 us
    pallas_call x1, Pallas kernels: 18.6 us -> 17.7 us  [shards(): pl.pallas_call(kernel, out_shape=jax.ShapeDtypeStruct((4, YB, XB), F32),...]
where the time goes in v7:
time: 19.4 us; the launch traced here: 19.3 us
  Pallas kernels  17.7 us (91%)
  local copies, waits for them, and re-layouts  1.57 us (8%)
    pallas_call x1, Pallas kernels, shards(): pl.pallas_call(kernel, out_shape=jax.ShapeDtypeStruct((4, YB, XB), F32),...  17.7 us
    unnamed x1, local copies, waits for them, and re-layouts  1.57 us

profile of v7, /device:TPU:97, one launch (start us, length us, event | category | flops | bytes accessed | tf_op | source)
XLA Modules:
  0.0 19.3 jit_solution(12294632644924339612)
XLA Ops:
  0.0 17.7 %render.1 = f32[4,64,64]{2,1,0:T(8,128)} custom-call(bf16[4,64,1024]{2,1,0:T(8,128)(2,1)} %vol.1, s32[64,1024]{1,0:T(8,128)} %entry.1, f32[4,256]{1,0:T(4,128)} %bitcast.1), custom_call_target="tpu_custom_call" | custom-call | tf_op jit(solution)/shard_map/render/pallas_call | solution.py:374
  17.7 1.6 %copy.5 = f32[4,64,64]{2,1,0:T(8,128)} copy(f32[4,64,64]{2,1,0:T(8,128)} %render.1) | data formatting | bytes 131072

commit v8 on v7

--- a/solution.py
+++ b/solution.py
@@ -75,8 +75,8 @@
 
 
 def kernel(
-    vol, entry, table, out,
-    vbuf, ebuf, tbuf, pk, hk, ck, rb, hb, cb, hcb, words, ent, band, side_band, pair, edges, sbuf, result,
+    vol, entry, table, result,
+    vbuf, ebuf, tbuf, pk, hk, ck, rb, hb, cb, hcb, words, ent, band, side_band, pair, edges, sbuf,
     vsem, esem, tsem, bsend, hsend, csend, brecv, hrecv, crecv, go,
 ):
     me = lax.axis_index("depth")
@@ -117,16 +117,16 @@
                 pair = halves(vbuf[z, x : x + 2 * XT, lanes], vbuf[z, XH + x : XH + x + 2 * XT, lanes], low)
                 for odd, v in enumerate(pair):
                     for c in range(2):
-                        pk[(first_chunk + c) * ND + 2 * g + odd, XT * z : XT * (z + 1), :] = v[XT * c : XT * (c + 1)]
-
-    def send_chunk(c):
+                        pk[first_chunk + c, 2 * g + odd, XT * z : XT * (z + 1), :] = v[XT * c : XT * (c + 1)]
+
+    def send_chunk(c, n=1):
         here = pl.ds(pl.multiple_of(CHUNK * me, CHUNK), CHUNK)
         for k in FAR_FIRST:
             pltpu.make_async_remote_copy(
-                pk.at[c * ND + (me ^ k)], rb.at[c, here, :], bsend, brecv.at[c],
+                pk.at[pl.ds(c, n), me ^ k], rb.at[pl.ds(c, n), here, :], bsend, brecv.at[c],
                 device_id={"img": im, "depth": me ^ k}, device_id_type=MESH,
             ).start()
-        pltpu.make_async_copy(pk.at[c * ND + me], rb.at[c, here, :], brecv.at[c]).start()
+        pltpu.make_async_copy(pk.at[pl.ds(c, n), me], rb.at[pl.ds(c, n), here, :], brecv.at[c]).start()
 
     load(0, firsts[0]).wait()
     load(1, firsts[1]).wait()
@@ -211,13 +211,12 @@
         ).start()
     pltpu.make_async_copy(hk.at[me], hb.at[tile_here, :], hrecv).start()
 
-    send_chunk(3)
-    send_chunk(2)
+    send_chunk(2, 2)
 
     @pl.when(has_left)
     def _():
         pl.semaphore_wait(go, 1)
-        for k in range(ND):
+        for k in FAR_FIRST + [0]:
             pltpu.make_async_remote_copy(
                 ck.at[me ^ k], cb.at[tile_here, :], csend, crecv,
                 device_id={"img": left, "depth": me ^ k}, device_id_type=MESH,
@@ -280,8 +279,8 @@
             values.append(b + away * (x - b))
         return values
 
-    def wait_chunk(c):
-        here = rb.at[c, pl.ds(0, ND * CHUNK), :]
+    def wait_chunk(c, n=1):
+        here = rb.at[pl.ds(c, n), pl.ds(0, ND * CHUNK), :]
         pltpu.make_async_copy(here, here, brecv.at[c]).wait()
 
     def store_sums(g, t, s):
@@ -299,8 +298,7 @@
             front, back = make_edges(pair[0:XH, :], pair[XH:XB, :], hb[...], low32)
             for t in range(NC - 1):
                 place_edges(t, front[XT * t : XT * (t + 1)], back[XT * t : XT * (t + 1)])
-            wait_chunk(3)
-            wait_chunk(2)
+            wait_chunk(2, 2)
 
         @pl.when(o == 1)
         def _():
@@ -354,12 +352,7 @@
         return 0
 
     lax.fori_loop(0, NC, column_tile, 0)
-    turned = result[...].reshape(4 * XH, LANES).T
-    for c in range(4):
-        for h in range(2):
-            out[c, :, XH * h : XH * (h + 1)] = turned[YB * h : YB * (h + 1), XH * c : XH * (c + 1)]
-
-    sent = pk.at[pl.ds(0, NC * (ND - 1))]
+    sent = pk.at[:, pl.ds(0, ND - 1)]
     pltpu.make_async_copy(sent, sent, bsend).wait()
     tiles = hk.at[pl.ds(0, ND - 1)]
     pltpu.make_async_copy(tiles, tiles, hsend).wait()
@@ -371,9 +364,9 @@
 
 def shards(volume, entry_depth, tf_table):
     dma = pltpu.SemaphoreType.DMA
-    return pl.pallas_call(
+    planes = pl.pallas_call(
         kernel,
-        out_shape=jax.ShapeDtypeStruct((4, YB, XB), F32),
+        out_shape=jax.ShapeDtypeStruct((4, XH, LANES), F32),
         in_specs=[
             pl.BlockSpec(memory_space=pl.ANY),
             pl.BlockSpec(memory_space=pl.ANY),
@@ -384,7 +377,7 @@
             pltpu.VMEM((ZB, XB, NY), BF16),
             pltpu.VMEM((XB, LANES), I32),
             pltpu.VMEM((4, 2 * LANES), F32),
-            pltpu.VMEM((NC * ND, CHUNK, LANES), BF16),
+            pltpu.VMEM((NC, ND, CHUNK, LANES), BF16),
             pltpu.VMEM((ND, TILE, LANES), BF16),
             pltpu.VMEM((ND, TILE, LANES), BF16),
             pltpu.VMEM((NC, (ND + 1) * CHUNK, LANES), BF16),
@@ -398,13 +391,13 @@
             pltpu.VMEM((XB, LANES), BF16),
             pltpu.VMEM((NC, NZ, XT, LANES), F32),
             pltpu.VMEM((NZ, XT, LANES), F32),
-            pltpu.VMEM((4, XH, LANES), F32),
             dma((4,)), dma, dma, dma, dma, dma,
             dma((NC,)), dma, dma, pltpu.SemaphoreType.REGULAR,
         ],
         compiler_params=pltpu.CompilerParams(collective_id=0, has_side_effects=True),
         name="render",
     )(volume, entry_depth, tf_table.T)
+    return planes.reshape(4, XH, 2, YB).transpose(0, 3, 2, 1).reshape(4, YB, XB)
 
 
 def solution(mesh):

time: 19.4 us -> 19.3 us (level)
  Pallas kernels: 17.7 us -> 17.4 us
    reshape x0 -> x3, local copies, waits for them, and re-layouts: none -> 1.73 us  [shards(): return planes.reshape(4, XH, 2, YB).transpose(0, 3, 2, 1).reshape(4, YB, XB)]
    unnamed x1 -> x0, local copies, waits for them, and re-layouts: 1.57 us -> none
    pallas_call x1, Pallas kernels: 17.7 us -> 17.4 us  [shards(): pl.pallas_call(kernel, out_shape=jax.ShapeDtypeStruct((4, XH, LANES), F32...]
where the time goes in v8:
time: 19.3 us; the launch traced here: 19.1 us
  Pallas kernels  17.4 us (90%)
  local copies, waits for them, and re-layouts  1.73 us (9%)
    pallas_call x1, Pallas kernels, shards(): pl.pallas_call(kernel, out_shape=jax.ShapeDtypeStruct((4, XH, LANES), F32...  17.4 us
    reshape x3, local copies, waits for them, and re-layouts, shards(): return planes.reshape(4, XH, 2, YB).transpose(0, 3, 2, 1).reshape(4, YB, XB)  1.73 us

profile of v8, /device:TPU:97, one launch (start us, length us, event | category | flops | bytes accessed | tf_op | source)
XLA Modules:
  0.0 19.1 jit_solution(9158183916945950252)
XLA Ops:
  0.0 17.4 %render.1 = f32[4,32,128]{2,1,0:T(8,128)} custom-call(bf16[4,64,1024]{2,1,0:T(8,128)(2,1)} %vol.1, s32[64,1024]{1,0:T(8,128)} %entry.1, f32[4,256]{1,0:T(4,128)} %bitcast.5), custom_call_target="tpu_custom_call" | custom-call | tf_op jit(solution)/shard_map/render/pallas_call | solution.py:367
  17.4 1.0 %reshape.6 = f32[4,32,2,64]{3,2,1,0:T(2,128)S(1)} reshape(f32[4,32,128]{2,1,0:T(8,128)} %render.1) | data formatting | bytes 131072 | tf_op jit(solution)/shard_map/reshape | solution.py:400
  18.4 0.8 %copy.6 = f32[4,64,64]{2,1,0:T(8,128)} copy(f32[4,64,64]{1,2,0:T(8,128)S(1)} %bitcast.4) | data formatting | bytes 131072 | tf_op jit(solution)/shard_map/reshape | solution.py:400
  (1 shorter events, 0.0 us)
